TPU v7x, 512 devices: a whole 4x8x8 slice. The times are simulated.
512 devices in a mesh: off: 2 (over x_hi), il: 8 (over y), xl: 32 (over x_lo, z, core).
Axes of the slice: x: 4 (x_hi: 2, x_lo: 2; x = x_hi * 2 + x_lo), y: 8, z: 8, core: 2. Of those that a mesh axis runs over, the one named last changes fastest.
Arguments:
- data: float32 [32, 128, 16, 1024], P('il', 'xl', 'off'), may hold values from -6 to 6
- offset_weight: float32 [16], P('off'), may hold values from 0.2 to 5
Outputs:
- slope: float32 [32, 128, 16, 1024], P('il', 'xl', 'off')
- stacked: float32 [32, 128, 1024], P('il', 'xl')
All inputs are finite; a program needn't handle non-finite values.
Results may differ from a plain program's by a relative error of at most 0.0003.
Values sent between devices are 32-bit elements; how exact they have to be, the bound alone decides.
A program may use at most 64 MiB of HBM per device.

v0:
```python
import jax
import jax.numpy as jnp
from jax import lax
from jax.sharding import PartitionSpec as P

ITERS = 3


damping = 0.05


def extended(block, sides, width):
    for axis, dim in sides:
        count = lax.axis_size(axis)
        forward = [(i, i + 1) for i in range(count - 1)]
        backward = [(target, source) for source, target in forward]
        low = lax.ppermute(
            lax.slice_in_dim(block, block.shape[dim] - width, None, axis=dim), axis, forward
        )
        high = lax.ppermute(lax.slice_in_dim(block, 0, width, axis=dim), axis, backward)
        block = jnp.concatenate([low, block, high], axis=dim)
    return block


def passed_along(x, axis, by):
    devices = lax.axis_size(axis)
    pairs = [(i, i + by) for i in range(devices) if 0 <= i + by < devices]
    return lax.ppermute(x, axis, pairs)


def weighted_box(padded, axis):
    length = padded.shape[axis] - 2
    left = lax.slice_in_dim(padded, 0, length, axis=axis)
    middle = lax.slice_in_dim(padded, 1, length + 1, axis=axis)
    right = lax.slice_in_dim(padded, 2, length + 2, axis=axis)
    return 0.25 * left + 0.5 * middle + 0.25 * right


def padded_along(field, axis):
    widths = [(0, 0)] * field.ndim
    widths[axis] = (1, 1)
    return jnp.pad(field, widths)


def smooth(field):
    field = weighted_box(padded_along(field, 3), 3)
    padded = extended(field, (("off", 2), ("il", 0), ("xl", 1)), 1)
    padded = weighted_box(padded, 0)
    padded = weighted_box(padded, 1)
    return weighted_box(padded, 2)


def time_derivative(field):
    padded = padded_along(field, 3)
    return 0.5 * (padded[..., 2:] - padded[..., :-2])


def move_gather(item):
    traces, places = item
    samples = traces.shape[1]
    block = min(samples, 128)
    outputs = jnp.arange(samples, dtype=jnp.float32)

    def add_block(turn, total):
        start = turn * block
        piece = lax.dynamic_slice_in_dim(traces, start, block, 1)
        where = lax.dynamic_slice_in_dim(places, start, block, 1)
        weights = jnp.maximum(0.0, 1.0 - jnp.abs(where[:, :, None] - outputs[None, None, :]))
        return total + jnp.sum(piece[:, :, None] * weights, axis=1)

    empty = jnp.zeros(traces.shape, jnp.float32)
    return lax.fori_loop(0, samples // block, add_block, empty)


def shards(data, offset_weight):
    local_offsets = data.shape[2]
    samples = data.shape[3]
    next_rows = passed_along(data[:, :, :1, :], "off", -1)
    following = jnp.concatenate([data[:, :, 1:, :], next_rows], axis=2)
    residual = following - data
    gradient = 0.5 * (time_derivative(data) + time_derivative(following))
    denominator = smooth(gradient * gradient) + damping
    slope = jnp.zeros_like(data)
    for step in range(ITERS):
        slope = slope - smooth(gradient * (residual + slope * gradient)) / denominator
    first_offset = (lax.axis_index("off") * local_offsets).astype(jnp.float32)
    times = jnp.arange(samples, dtype=jnp.float32) + 1.0
    offsets = jnp.arange(local_offsets, dtype=jnp.float32) + 0.5 + first_offset
    squared = times * times - times * offsets[:, None] * slope
    target = jnp.sqrt(jnp.maximum(squared, 1.0)) - 1.0
    midpoints = data.shape[0] * data.shape[1]
    traces = data.reshape(midpoints, local_offsets, samples)
    places = target.reshape(midpoints, local_offsets, samples)
    corrected = lax.map(move_gather, (traces, places)).reshape(data.shape)
    partial_stack = jnp.sum(corrected * offset_weight[None, None, :, None], axis=2)
    stack_total, weight_sum = lax.psum((partial_stack, jnp.sum(offset_weight)), "off")
    stacked = stack_total / weight_sum
    return (slope, stacked)


def solution(mesh):
    return jax.shard_map(
        shards,
        mesh=mesh,
        in_specs=(P("il", "xl", "off", None), P("off")),
        out_specs=(P("il", "xl", "off", None), P("il", "xl", None)),
        check_vma=False,
    )
```

profile of v0, /device:TPU:1, one launch (start us, length us, event | category | flops | bytes accessed | tf_op | source)
XLA Modules:
  0.0 339.6 jit_solution(5269974631932482849)
XLA Ops:
  10.8 4.1 %collective-permute-done = f32[4,4,1,1024]{3,2,1,0:T(1,128)S(1)} collective-permute-done((f32[4,4,1,1024]{3,2,1,0:T(1,128)S(1)}, f32[4,4,1,1024]{3,2,1,0:T(1,128)S(1)}, u32[]{:S(2)}, u32[]{:S(2)}) %collective-permute-start) | collective-permute-done | bytes 65568 | tf_op jit(solution)/shard_map/ppermute | solution.py:28
  19.4 5.5 %collective-permute-start.1 = (f32[4,4,1,1024]{3,2,1,0:T(1,128)S(1)}, f32[4,4,1,1024]{3,2,1,0:T(1,128)S(1)}, u32[]{:S(2)}, u32[]{:S(2)}) collective-permute-start(f32[4,4,1,1024]{3,2,1,0:T(1,128)S(1)} %get-tuple-element.187), channel_id=1, source_target_pairs={{0,256},{1,257},{2,258},{3,259},{4,260},{5,261},{6,262},{7,263},{8... | collective-permute-start | bytes 196616 | tf_op jit(solution)/shard_map/ppermute | solution.py:17
  27.6 4.7 %collective-permute-start.9 = (f32[1,4,10,1024]{3,2,1,0:T(8,128)S(1)}, f32[1,4,10,1024]{3,2,1,0:T(8,128)S(1)}, u32[]{:S(2)}, u32[]{:S(2)}) collective-permute-start(f32[1,4,10,1024]{3,2,1,0:T(8,128)S(1)} %get-tuple-element.177), channel_id=1, source_target_pairs={{0,32},{32,64},{64,96},{96,128},{128,160},{160,192},{192,224},{1,3... | collective-permute-start | bytes 491528 | tf_op jit(solution)/shard_map/ppermute | solution.py:17
  37.2 8.6 %collective-permute-start.11 = (f32[6,1,10,1024]{3,2,1,0:T(8,128)S(1)}, f32[6,1,10,1024]{3,2,1,0:T(8,128)S(1)}, u32[]{:S(2)}, u32[]{:S(2)}) collective-permute-start(f32[6,1,10,1024]{3,2,1,0:T(8,128)S(1)} %get-tuple-element.169), channel_id=1, source_target_pairs={{0,1},{1,2},{2,3},{3,4},{4,5},{5,6},{6,7},{7,8},{8,9},{9,10},{10,1... | collective-permute-start | bytes 737288 | tf_op jit(solution)/shard_map/ppermute | solution.py:17
  56.3 4.4 %collective-permute-done.6 = f32[6,1,10,1024]{3,2,1,0:T(8,128)S(1)} collective-permute-done((f32[6,1,10,1024]{3,2,1,0:T(8,128)S(1)}, f32[6,1,10,1024]{3,2,1,0:T(8,128)S(1)}, u32[]{:S(2)}, u32[]{:S(2)}) %collective-permute-start.6) | collective-permute-done | bytes 245792 | tf_op jit(solution)/shard_map/ppermute | solution.py:20
  62.5 5.9 %collective-permute-start.13 = (f32[4,4,1,1024]{3,2,1,0:T(1,128)S(1)}, f32[4,4,1,1024]{3,2,1,0:T(1,128)S(1)}, u32[]{:S(2)}, u32[]{:S(2)}) collective-permute-start(f32[4,4,1,1024]{3,2,1,0:T(1,128)S(1)} %get-tuple-element.183), channel_id=1, source_target_pairs={{0,256},{1,257},{2,258},{3,259},{4,260},{5,261},{6,262},{7,263},{8... | collective-permute-start | bytes 196616 | tf_op jit(solution)/shard_map/ppermute | solution.py:17
  69.7 5.2 %collective-permute-done.14 = f32[4,4,1,1024]{3,2,1,0:T(1,128)S(1)} collective-permute-done((f32[4,4,1,1024]{3,2,1,0:T(1,128)S(1)}, f32[4,4,1,1024]{3,2,1,0:T(1,128)S(1)}, u32[]{:S(2)}, u32[]{:S(2)}) %collective-permute-start.14) | collective-permute-done | bytes 65568 | tf_op jit(solution)/shard_map/ppermute | solution.py:20
  86.3 7.4 %collective-permute-start.17 = (f32[6,1,10,1024]{3,2,1,0:T(8,128)S(1)}, f32[6,1,10,1024]{3,2,1,0:T(8,128)S(1)}, u32[]{:S(2)}, u32[]{:S(2)}) collective-permute-start(f32[6,1,10,1024]{3,2,1,0:T(8,128)S(1)} %get-tuple-element.167), channel_id=1, source_target_pairs={{0,1},{1,2},{2,3},{3,4},{4,5},{5,6},{6,7},{7,8},{8,9},{9,10},{10,1... | collective-permute-start | bytes 737288 | tf_op jit(solution)/shard_map/ppermute | solution.py:17
  98.4 4.4 %collective-permute-done.18 = f32[6,1,10,1024]{3,2,1,0:T(8,128)S(1)} collective-permute-done((f32[6,1,10,1024]{3,2,1,0:T(8,128)S(1)}, f32[6,1,10,1024]{3,2,1,0:T(8,128)S(1)}, u32[]{:S(2)}, u32[]{:S(2)}) %collective-permute-start.18) | collective-permute-done | bytes 245792 | tf_op jit(solution)/shard_map/ppermute | solution.py:20
  107.2 5.2 %collective-permute-done.20 = f32[4,4,1,1024]{3,2,1,0:T(1,128)S(1)} collective-permute-done((f32[4,4,1,1024]{3,2,1,0:T(1,128)S(1)}, f32[4,4,1,1024]{3,2,1,0:T(1,128)S(1)}, u32[]{:S(2)}, u32[]{:S(2)}) %collective-permute-start.20) | collective-permute-done | bytes 65568 | tf_op jit(solution)/shard_map/ppermute | solution.py:20
  119.4 5.0 %collective-permute-done.22 = f32[1,4,10,1024]{3,2,1,0:T(8,128)S(1)} collective-permute-done((f32[1,4,10,1024]{3,2,1,0:T(8,128)S(1)}, f32[1,4,10,1024]{3,2,1,0:T(8,128)S(1)}, u32[]{:S(2)}, u32[]{:S(2)}) %collective-permute-start.22) | collective-permute-done | bytes 163872 | tf_op jit(solution)/shard_map/ppermute | solution.py:20
  125.4 6.6 %collective-permute-start.23 = (f32[6,1,10,1024]{3,2,1,0:T(8,128)}, f32[6,1,10,1024]{3,2,1,0:T(8,128)}, u32[]{:S(2)}, u32[]{:S(2)}) collective-permute-start(f32[6,1,10,1024]{3,2,1,0:T(8,128)} %get-tuple-element.165), channel_id=1, source_target_pairs={{0,1},{1,2},{2,3},{3,4},{4,5},{5,6},{6,7},{7,8},{8,9},{9,10},{10,1... | collective-permute-start | bytes 737288 | tf_op jit(solution)/shard_map/ppermute | solution.py:17
  137.0 4.4 %collective-permute-done.24 = f32[6,1,10,1024]{3,2,1,0:T(8,128)} collective-permute-done((f32[6,1,10,1024]{3,2,1,0:T(8,128)}, f32[6,1,10,1024]{3,2,1,0:T(8,128)}, u32[]{:S(2)}, u32[]{:S(2)}) %collective-permute-start.24) | collective-permute-done | bytes 245792 | tf_op jit(solution)/shard_map/ppermute | solution.py:20
  144.5 144.8 %while.25 = (s32[]{:T(128)}, f32[16,8,1024]{2,1,0:T(8,128)S(1)}, f32[16,8,1024]{2,1,0:T(8,128)S(1)}, f32[16,8,1024]{2,1,0:T(8,128)S(1)}, s32[]{:T(128)}, /*index...) while((s32[]{:T(128)}, f32[16,8,1024]{2,1,0:T(8,128)S(1)}, f32[16,8,1024]{2,1,0:T(8,128)S(1)}, ...), condition=%wide.region_4.5_spmd, body=%wide.region_0.4_spmd.sunk | while | flops 6299657 | bytes 352582 | solution.py:94
  144.6 9.0 %while.26 = (s32[]{:T(128)}, f32[8,1024]{1,0:T(8,128)S(1)}, f32[8,1024]{1,0:T(8,128)S(1)}, f32[8,1024]{1,0:T(8,128)S(1)}, s32[]{:T(128)}, /*index=5*/s32[]{:T(128)}, s32[]{:T(128)}, s32[]{:T(128)}) while((s32[]{:T(128)}, f32[8,1024]{1,0:T(8,128)S(1)}, f32[8,1024]{1,0:T(8,128)S(1)}, f32[8,1024]{1,0:T(8,128)S(1)}, s32[]{:T(128)}, ...), condition=%wide.region_3.3_spmd.clone, body=%wide.region_1.2_spmd.clone.sunk | while | flops 6299655 | bytes 155793 | solution.py:72
  153.6 9.0 %while.26 = (s32[]{:T(128)}, f32[8,1024]{1,0:T(8,128)S(1)}, f32[8,1024]{1,0:T(8,128)S(1)}, f32[8,1024]{1,0:T(8,128)S(1)}, s32[]{:T(128)}, /*index=5*/s32[]{:T(128)}, s32[]{:T(128)}, s32[]{:T(128)}) while((s32[]{:T(128)}, f32[8,1024]{1,0:T(8,128)S(1)}, f32[8,1024]{1,0:T(8,128)S(1)}, f32[8,1024]{1,0:T(8,128)S(1)}, s32[]{:T(128)}, ...), condition=%wide.region_3.3_spmd.clone, body=%wide.region_1.2_spmd.clone.sunk | while | flops 6299655 | bytes 155793 | solution.py:72
  162.7 9.0 %while.26 = (s32[]{:T(128)}, f32[8,1024]{1,0:T(8,128)S(1)}, f32[8,1024]{1,0:T(8,128)S(1)}, f32[8,1024]{1,0:T(8,128)S(1)}, s32[]{:T(128)}, /*index=5*/s32[]{:T(128)}, s32[]{:T(128)}, s32[]{:T(128)}) while((s32[]{:T(128)}, f32[8,1024]{1,0:T(8,128)S(1)}, f32[8,1024]{1,0:T(8,128)S(1)}, f32[8,1024]{1,0:T(8,128)S(1)}, s32[]{:T(128)}, ...), condition=%wide.region_3.3_spmd.clone, body=%wide.region_1.2_spmd.clone.sunk | while | flops 6299655 | bytes 155793 | solution.py:72
  171.7 9.0 %while.26 = (s32[]{:T(128)}, f32[8,1024]{1,0:T(8,128)S(1)}, f32[8,1024]{1,0:T(8,128)S(1)}, f32[8,1024]{1,0:T(8,128)S(1)}, s32[]{:T(128)}, /*index=5*/s32[]{:T(128)}, s32[]{:T(128)}, s32[]{:T(128)}) while((s32[]{:T(128)}, f32[8,1024]{1,0:T(8,128)S(1)}, f32[8,1024]{1,0:T(8,128)S(1)}, f32[8,1024]{1,0:T(8,128)S(1)}, s32[]{:T(128)}, ...), condition=%wide.region_3.3_spmd.clone, body=%wide.region_1.2_spmd.clone.sunk | while | flops 6299655 | bytes 155793 | solution.py:72
  180.8 9.0 %while.26 = (s32[]{:T(128)}, f32[8,1024]{1,0:T(8,128)S(1)}, f32[8,1024]{1,0:T(8,128)S(1)}, f32[8,1024]{1,0:T(8,128)S(1)}, s32[]{:T(128)}, /*index=5*/s32[]{:T(128)}, s32[]{:T(128)}, s32[]{:T(128)}) while((s32[]{:T(128)}, f32[8,1024]{1,0:T(8,128)S(1)}, f32[8,1024]{1,0:T(8,128)S(1)}, f32[8,1024]{1,0:T(8,128)S(1)}, s32[]{:T(128)}, ...), condition=%wide.region_3.3_spmd.clone, body=%wide.region_1.2_spmd.clone.sunk | while | flops 6299655 | bytes 155793 | solution.py:72
  189.8 9.0 %while.26 = (s32[]{:T(128)}, f32[8,1024]{1,0:T(8,128)S(1)}, f32[8,1024]{1,0:T(8,128)S(1)}, f32[8,1024]{1,0:T(8,128)S(1)}, s32[]{:T(128)}, /*index=5*/s32[]{:T(128)}, s32[]{:T(128)}, s32[]{:T(128)}) while((s32[]{:T(128)}, f32[8,1024]{1,0:T(8,128)S(1)}, f32[8,1024]{1,0:T(8,128)S(1)}, f32[8,1024]{1,0:T(8,128)S(1)}, s32[]{:T(128)}, ...), condition=%wide.region_3.3_spmd.clone, body=%wide.region_1.2_spmd.clone.sunk | while | flops 6299655 | bytes 155793 | solution.py:72
  198.9 9.0 %while.26 = (s32[]{:T(128)}, f32[8,1024]{1,0:T(8,128)S(1)}, f32[8,1024]{1,0:T(8,128)S(1)}, f32[8,1024]{1,0:T(8,128)S(1)}, s32[]{:T(128)}, /*index=5*/s32[]{:T(128)}, s32[]{:T(128)}, s32[]{:T(128)}) while((s32[]{:T(128)}, f32[8,1024]{1,0:T(8,128)S(1)}, f32[8,1024]{1,0:T(8,128)S(1)}, f32[8,1024]{1,0:T(8,128)S(1)}, s32[]{:T(128)}, ...), condition=%wide.region_3.3_spmd.clone, body=%wide.region_1.2_spmd.clone.sunk | while | flops 6299655 | bytes 155793 | solution.py:72
  207.9 9.0 %while.26 = (s32[]{:T(128)}, f32[8,1024]{1,0:T(8,128)S(1)}, f32[8,1024]{1,0:T(8,128)S(1)}, f32[8,1024]{1,0:T(8,128)S(1)}, s32[]{:T(128)}, /*index=5*/s32[]{:T(128)}, s32[]{:T(128)}, s32[]{:T(128)}) while((s32[]{:T(128)}, f32[8,1024]{1,0:T(8,128)S(1)}, f32[8,1024]{1,0:T(8,128)S(1)}, f32[8,1024]{1,0:T(8,128)S(1)}, s32[]{:T(128)}, ...), condition=%wide.region_3.3_spmd.clone, body=%wide.region_1.2_spmd.clone.sunk | while | flops 6299655 | bytes 155793 | solution.py:72
  217.0 9.0 %while.26 = (s32[]{:T(128)}, f32[8,1024]{1,0:T(8,128)S(1)}, f32[8,1024]{1,0:T(8,128)S(1)}, f32[8,1024]{1,0:T(8,128)S(1)}, s32[]{:T(128)}, /*index=5*/s32[]{:T(128)}, s32[]{:T(128)}, s32[]{:T(128)}) while((s32[]{:T(128)}, f32[8,1024]{1,0:T(8,128)S(1)}, f32[8,1024]{1,0:T(8,128)S(1)}, f32[8,1024]{1,0:T(8,128)S(1)}, s32[]{:T(128)}, ...), condition=%wide.region_3.3_spmd.clone, body=%wide.region_1.2_spmd.clone.sunk | while | flops 6299655 | bytes 155793 | solution.py:72
  226.0 9.0 %while.26 = (s32[]{:T(128)}, f32[8,1024]{1,0:T(8,128)S(1)}, f32[8,1024]{1,0:T(8,128)S(1)}, f32[8,1024]{1,0:T(8,128)S(1)}, s32[]{:T(128)}, /*index=5*/s32[]{:T(128)}, s32[]{:T(128)}, s32[]{:T(128)}) while((s32[]{:T(128)}, f32[8,1024]{1,0:T(8,128)S(1)}, f32[8,1024]{1,0:T(8,128)S(1)}, f32[8,1024]{1,0:T(8,128)S(1)}, s32[]{:T(128)}, ...), condition=%wide.region_3.3_spmd.clone, body=%wide.region_1.2_spmd.clone.sunk | while | flops 6299655 | bytes 155793 | solution.py:72
  235.1 9.0 %while.26 = (s32[]{:T(128)}, f32[8,1024]{1,0:T(8,128)S(1)}, f32[8,1024]{1,0:T(8,128)S(1)}, f32[8,1024]{1,0:T(8,128)S(1)}, s32[]{:T(128)}, /*index=5*/s32[]{:T(128)}, s32[]{:T(128)}, s32[]{:T(128)}) while((s32[]{:T(128)}, f32[8,1024]{1,0:T(8,128)S(1)}, f32[8,1024]{1,0:T(8,128)S(1)}, f32[8,1024]{1,0:T(8,128)S(1)}, s32[]{:T(128)}, ...), condition=%wide.region_3.3_spmd.clone, body=%wide.region_1.2_spmd.clone.sunk | while | flops 6299655 | bytes 155793 | solution.py:72
  244.1 9.0 %while.26 = (s32[]{:T(128)}, f32[8,1024]{1,0:T(8,128)S(1)}, f32[8,1024]{1,0:T(8,128)S(1)}, f32[8,1024]{1,0:T(8,128)S(1)}, s32[]{:T(128)}, /*index=5*/s32[]{:T(128)}, s32[]{:T(128)}, s32[]{:T(128)}) while((s32[]{:T(128)}, f32[8,1024]{1,0:T(8,128)S(1)}, f32[8,1024]{1,0:T(8,128)S(1)}, f32[8,1024]{1,0:T(8,128)S(1)}, s32[]{:T(128)}, ...), condition=%wide.region_3.3_spmd.clone, body=%wide.region_1.2_spmd.clone.sunk | while | flops 6299655 | bytes 155793 | solution.py:72
  253.2 9.0 %while.26 = (s32[]{:T(128)}, f32[8,1024]{1,0:T(8,128)S(1)}, f32[8,1024]{1,0:T(8,128)S(1)}, f32[8,1024]{1,0:T(8,128)S(1)}, s32[]{:T(128)}, /*index=5*/s32[]{:T(128)}, s32[]{:T(128)}, s32[]{:T(128)}) while((s32[]{:T(128)}, f32[8,1024]{1,0:T(8,128)S(1)}, f32[8,1024]{1,0:T(8,128)S(1)}, f32[8,1024]{1,0:T(8,128)S(1)}, s32[]{:T(128)}, ...), condition=%wide.region_3.3_spmd.clone, body=%wide.region_1.2_spmd.clone.sunk | while | flops 6299655 | bytes 155793 | solution.py:72
  262.2 9.0 %while.26 = (s32[]{:T(128)}, f32[8,1024]{1,0:T(8,128)S(1)}, f32[8,1024]{1,0:T(8,128)S(1)}, f32[8,1024]{1,0:T(8,128)S(1)}, s32[]{:T(128)}, /*index=5*/s32[]{:T(128)}, s32[]{:T(128)}, s32[]{:T(128)}) while((s32[]{:T(128)}, f32[8,1024]{1,0:T(8,128)S(1)}, f32[8,1024]{1,0:T(8,128)S(1)}, f32[8,1024]{1,0:T(8,128)S(1)}, s32[]{:T(128)}, ...), condition=%wide.region_3.3_spmd.clone, body=%wide.region_1.2_spmd.clone.sunk | while | flops 6299655 | bytes 155793 | solution.py:72
  271.3 9.0 %while.26 = (s32[]{:T(128)}, f32[8,1024]{1,0:T(8,128)S(1)}, f32[8,1024]{1,0:T(8,128)S(1)}, f32[8,1024]{1,0:T(8,128)S(1)}, s32[]{:T(128)}, /*index=5*/s32[]{:T(128)}, s32[]{:T(128)}, s32[]{:T(128)}) while((s32[]{:T(128)}, f32[8,1024]{1,0:T(8,128)S(1)}, f32[8,1024]{1,0:T(8,128)S(1)}, f32[8,1024]{1,0:T(8,128)S(1)}, s32[]{:T(128)}, ...), condition=%wide.region_3.3_spmd.clone, body=%wide.region_1.2_spmd.clone.sunk | while | flops 6299655 | bytes 155793 | solution.py:72
  280.4 9.0 %while.26 = (s32[]{:T(128)}, f32[8,1024]{1,0:T(8,128)S(1)}, f32[8,1024]{1,0:T(8,128)S(1)}, f32[8,1024]{1,0:T(8,128)S(1)}, s32[]{:T(128)}, /*index=5*/s32[]{:T(128)}, s32[]{:T(128)}, s32[]{:T(128)}) while((s32[]{:T(128)}, f32[8,1024]{1,0:T(8,128)S(1)}, f32[8,1024]{1,0:T(8,128)S(1)}, f32[8,1024]{1,0:T(8,128)S(1)}, s32[]{:T(128)}, ...), condition=%wide.region_3.3_spmd.clone, body=%wide.region_1.2_spmd.clone.sunk | while | flops 6299655 | bytes 155793 | solution.py:72
  290.9 6.0 %psum.15 = f32[]{:T(128)} all-reduce(f32[]{:T(128)} %reduce_sum.35), channel_id=1, replica_groups=mesh['off'=2,'il'=8,'xl'=32] {'off'}, use_global_device_ids=true, to_apply=%region_8.9 | all-reduce | flops 1 | bytes 8 | tf_op jit(solution)/shard_map/psum | solution.py:96
  296.9 33.8 %all-reduce.8.cloned.1.call-done = f32[4,4,1024]{2,1,0:T(4,128)} async-done(((f32[4,4,1024]{2,1,0:T(4,128)}), f32[4,4,1024]{2,1,0:T(4,128)}) %all-reduce.8.cloned.1.call-update) | async-done | bytes 65552 | tf_op jit(solution)/shard_map/psum | solution.py:96
  (519 shorter events, 207.0 us)
Async XLA Ops:
  7.2 7.8 %copy-start = (f32[4,4,8,1024]{3,2,1,0:T(8,128)S(1)}, f32[4,4,8,1024]{3,2,1,0:T(8,128)}, u32[]{:S(2)}) copy-start(f32[4,4,8,1024]{3,2,1,0:T(8,128)} %param.6) | copy-start | bytes 1572868
  7.2 323.5 %all-reduce.8.cloned.1.call-start = ((), (), s32[]{:S(2)}) async-start(), calls=%async_computation | async-start | bytes 131072 | tf_op jit(solution)/shard_map/psum | solution.py:96
  8.3 6.5 %collective-permute-start = (f32[4,4,1,1024]{3,2,1,0:T(1,128)S(1)}, f32[4,4,1,1024]{3,2,1,0:T(1,128)S(1)}, u32[]{:S(2)}, u32[]{:S(2)}) collective-permute-start(f32[4,4,1,1024]{3,2,1,0:T(1,128)S(1)} %slice.229), channel_id=1, source_target_pairs={{256,0},{257,1},{258,2},{259,3},{260,4},{261,5},{262,6},{263,7},{2... | collective-permute-start | bytes 196616 | tf_op jit(solution)/shard_map/ppermute | solution.py:28
  16.4 9.8 %collective-permute-start.7 = (f32[4,4,1,1024]{3,2,1,0:T(1,128)S(1)}, f32[4,4,1,1024]{3,2,1,0:T(1,128)S(1)}, u32[]{:S(2)}, u32[]{:S(2)}) collective-permute-start(f32[4,4,1,1024]{3,2,1,0:T(1,128)S(1)} %get-tuple-element.185), channel_id=1, source_target_pairs={{0,256},{1,257},{2,258},{3,259},{4,260},{5,261},{6,262},{7,263},{8... | collective-permute-start | bytes 196616 | tf_op jit(solution)/shard_map/ppermute | solution.py:17
  18.0 8.2 %collective-permute-start.8 = (f32[4,4,1,1024]{3,2,1,0:T(1,128)S(1)}, f32[4,4,1,1024]{3,2,1,0:T(1,128)S(1)}, u32[]{:S(2)}, u32[]{:S(2)}) collective-permute-start(f32[4,4,1,1024]{3,2,1,0:T(1,128)S(1)} %get-tuple-element.186), channel_id=1, source_target_pairs={{256,0},{257,1},{258,2},{259,3},{260,4},{261,5},{262,6},{263,7},{2... | collective-permute-start | bytes 196616 | tf_op jit(solution)/shard_map/ppermute | solution.py:20
  19.4 12.9 %collective-permute-start.1 = (f32[4,4,1,1024]{3,2,1,0:T(1,128)S(1)}, f32[4,4,1,1024]{3,2,1,0:T(1,128)S(1)}, u32[]{:S(2)}, u32[]{:S(2)}) collective-permute-start(f32[4,4,1,1024]{3,2,1,0:T(1,128)S(1)} %get-tuple-element.187), channel_id=1, source_target_pairs={{0,256},{1,257},{2,258},{3,259},{4,260},{5,261},{6,262},{7,263},{8... | collective-permute-start | bytes 196616 | tf_op jit(solution)/shard_map/ppermute | solution.py:17
  24.9 7.4 %collective-permute-start.2 = (f32[4,4,1,1024]{3,2,1,0:T(1,128)S(1)}, f32[4,4,1,1024]{3,2,1,0:T(1,128)S(1)}, u32[]{:S(2)}, u32[]{:S(2)}) collective-permute-start(f32[4,4,1,1024]{3,2,1,0:T(1,128)S(1)} %get-tuple-element.188), channel_id=1, source_target_pairs={{256,0},{257,1},{258,2},{259,3},{260,4},{261,5},{262,6},{263,7},{2... | collective-permute-start | bytes 196616 | tf_op jit(solution)/shard_map/ppermute | solution.py:20
  26.3 10.8 %collective-permute-start.10 = (f32[1,4,10,1024]{3,2,1,0:T(8,128)S(1)}, f32[1,4,10,1024]{3,2,1,0:T(8,128)S(1)}, u32[]{:S(2)}, u32[]{:S(2)}) collective-permute-start(f32[1,4,10,1024]{3,2,1,0:T(8,128)S(1)} %get-tuple-element.178), channel_id=1, source_target_pairs={{32,0},{64,32},{96,64},{128,96},{160,128},{192,160},{224,192},{33,... | collective-permute-start | bytes 491528 | tf_op jit(solution)/shard_map/ppermute | solution.py:20
  27.6 9.5 %collective-permute-start.9 = (f32[1,4,10,1024]{3,2,1,0:T(8,128)S(1)}, f32[1,4,10,1024]{3,2,1,0:T(8,128)S(1)}, u32[]{:S(2)}, u32[]{:S(2)}) collective-permute-start(f32[1,4,10,1024]{3,2,1,0:T(8,128)S(1)} %get-tuple-element.177), channel_id=1, source_target_pairs={{0,32},{32,64},{64,96},{96,128},{128,160},{160,192},{192,224},{1,3... | collective-permute-start | bytes 491528 | tf_op jit(solution)/shard_map/ppermute | solution.py:17
  32.4 16.5 %collective-permute-start.3 = (f32[1,4,10,1024]{3,2,1,0:T(8,128)S(1)}, f32[1,4,10,1024]{3,2,1,0:T(8,128)S(1)}, u32[]{:S(2)}, u32[]{:S(2)}) collective-permute-start(f32[1,4,10,1024]{3,2,1,0:T(8,128)S(1)} %get-tuple-element.179), channel_id=1, source_target_pairs={{0,32},{32,64},{64,96},{96,128},{128,160},{160,192},{192,224},{1,3... | collective-permute-start | bytes 491528 | tf_op jit(solution)/shard_map/ppermute | solution.py:17
  35.8 13.2 %collective-permute-start.4 = (f32[1,4,10,1024]{3,2,1,0:T(8,128)S(1)}, f32[1,4,10,1024]{3,2,1,0:T(8,128)S(1)}, u32[]{:S(2)}, u32[]{:S(2)}) collective-permute-start(f32[1,4,10,1024]{3,2,1,0:T(8,128)S(1)} %get-tuple-element.180), channel_id=1, source_target_pairs={{32,0},{64,32},{96,64},{128,96},{160,128},{192,160},{224,192},{33,... | collective-permute-start | bytes 491528 | tf_op jit(solution)/shard_map/ppermute | solution.py:20
  37.2 17.2 %collective-permute-start.11 = (f32[6,1,10,1024]{3,2,1,0:T(8,128)S(1)}, f32[6,1,10,1024]{3,2,1,0:T(8,128)S(1)}, u32[]{:S(2)}, u32[]{:S(2)}) collective-permute-start(f32[6,1,10,1024]{3,2,1,0:T(8,128)S(1)} %get-tuple-element.169), channel_id=1, source_target_pairs={{0,1},{1,2},{2,3},{3,4},{4,5},{5,6},{6,7},{7,8},{8,9},{9,10},{10,1... | collective-permute-start | bytes 737288 | tf_op jit(solution)/shard_map/ppermute | solution.py:17
  45.8 9.1 %collective-permute-start.12 = (f32[6,1,10,1024]{3,2,1,0:T(8,128)S(1)}, f32[6,1,10,1024]{3,2,1,0:T(8,128)S(1)}, u32[]{:S(2)}, u32[]{:S(2)}) collective-permute-start(f32[6,1,10,1024]{3,2,1,0:T(8,128)S(1)} %get-tuple-element.170), channel_id=1, source_target_pairs={{1,0},{2,1},{3,2},{4,3},{5,4},{6,5},{7,6},{8,7},{9,8},{10,9},{11,1... | collective-permute-start | bytes 737288 | tf_op jit(solution)/shard_map/ppermute | solution.py:20
  49.1 7.2 %collective-permute-start.5 = (f32[6,1,10,1024]{3,2,1,0:T(8,128)S(1)}, f32[6,1,10,1024]{3,2,1,0:T(8,128)S(1)}, u32[]{:S(2)}, u32[]{:S(2)}) collective-permute-start(f32[6,1,10,1024]{3,2,1,0:T(8,128)S(1)} %get-tuple-element.171), channel_id=1, source_target_pairs={{0,1},{1,2},{2,3},{3,4},{4,5},{5,6},{6,7},{7,8},{8,9},{9,10},{10,1... | collective-permute-start | bytes 737288 | tf_op jit(solution)/shard_map/ppermute | solution.py:17
  51.6 9.1 %collective-permute-start.6 = (f32[6,1,10,1024]{3,2,1,0:T(8,128)S(1)}, f32[6,1,10,1024]{3,2,1,0:T(8,128)S(1)}, u32[]{:S(2)}, u32[]{:S(2)}) collective-permute-start(f32[6,1,10,1024]{3,2,1,0:T(8,128)S(1)} %get-tuple-element.172), channel_id=1, source_target_pairs={{1,0},{2,1},{3,2},{4,3},{5,4},{6,5},{7,6},{8,7},{9,8},{10,9},{11,1... | collective-permute-start | bytes 737288 | tf_op jit(solution)/shard_map/ppermute | solution.py:20
  62.5 7.2 %collective-permute-start.13 = (f32[4,4,1,1024]{3,2,1,0:T(1,128)S(1)}, f32[4,4,1,1024]{3,2,1,0:T(1,128)S(1)}, u32[]{:S(2)}, u32[]{:S(2)}) collective-permute-start(f32[4,4,1,1024]{3,2,1,0:T(1,128)S(1)} %get-tuple-element.183), channel_id=1, source_target_pairs={{0,256},{1,257},{2,258},{3,259},{4,260},{5,261},{6,262},{7,263},{8... | collective-permute-start | bytes 196616 | tf_op jit(solution)/shard_map/ppermute | solution.py:17
  68.4 6.5 %collective-permute-start.14 = (f32[4,4,1,1024]{3,2,1,0:T(1,128)S(1)}, f32[4,4,1,1024]{3,2,1,0:T(1,128)S(1)}, u32[]{:S(2)}, u32[]{:S(2)}) collective-permute-start(f32[4,4,1,1024]{3,2,1,0:T(1,128)S(1)} %get-tuple-element.184), channel_id=1, source_target_pairs={{256,0},{257,1},{258,2},{259,3},{260,4},{261,5},{262,6},{263,7},{2... | collective-permute-start | bytes 196616 | tf_op jit(solution)/shard_map/ppermute | solution.py:20
  75.0 7.4 %collective-permute-start.15 = (f32[1,4,10,1024]{3,2,1,0:T(8,128)S(1)}, f32[1,4,10,1024]{3,2,1,0:T(8,128)S(1)}, u32[]{:S(2)}, u32[]{:S(2)}) collective-permute-start(f32[1,4,10,1024]{3,2,1,0:T(8,128)S(1)} %get-tuple-element.175), channel_id=1, source_target_pairs={{0,32},{32,64},{64,96},{96,128},{128,160},{160,192},{192,224},{1,3... | collective-permute-start | bytes 491528 | tf_op jit(solution)/shard_map/ppermute | solution.py:17
  79.1 7.1 %collective-permute-start.16 = (f32[1,4,10,1024]{3,2,1,0:T(8,128)S(1)}, f32[1,4,10,1024]{3,2,1,0:T(8,128)S(1)}, u32[]{:S(2)}, u32[]{:S(2)}) collective-permute-start(f32[1,4,10,1024]{3,2,1,0:T(8,128)S(1)} %get-tuple-element.176), channel_id=1, source_target_pairs={{32,0},{64,32},{96,64},{128,96},{160,128},{192,160},{224,192},{33,... | collective-permute-start | bytes 491528 | tf_op jit(solution)/shard_map/ppermute | solution.py:20
  86.3 12.1 %collective-permute-start.17 = (f32[6,1,10,1024]{3,2,1,0:T(8,128)S(1)}, f32[6,1,10,1024]{3,2,1,0:T(8,128)S(1)}, u32[]{:S(2)}, u32[]{:S(2)}) collective-permute-start(f32[6,1,10,1024]{3,2,1,0:T(8,128)S(1)} %get-tuple-element.167), channel_id=1, source_target_pairs={{0,1},{1,2},{2,3},{3,4},{4,5},{5,6},{6,7},{7,8},{8,9},{9,10},{10,1... | collective-permute-start | bytes 737288 | tf_op jit(solution)/shard_map/ppermute | solution.py:17
  93.7 9.1 %collective-permute-start.18 = (f32[6,1,10,1024]{3,2,1,0:T(8,128)S(1)}, f32[6,1,10,1024]{3,2,1,0:T(8,128)S(1)}, u32[]{:S(2)}, u32[]{:S(2)}) collective-permute-start(f32[6,1,10,1024]{3,2,1,0:T(8,128)S(1)} %get-tuple-element.168), channel_id=1, source_target_pairs={{1,0},{2,1},{3,2},{4,3},{5,4},{6,5},{7,6},{8,7},{9,8},{10,9},{11,1... | collective-permute-start | bytes 737288 | tf_op jit(solution)/shard_map/ppermute | solution.py:20
  104.6 2.6 collective-permute-start.19
  105.9 6.5 %collective-permute-start.20 = (f32[4,4,1,1024]{3,2,1,0:T(1,128)S(1)}, f32[4,4,1,1024]{3,2,1,0:T(1,128)S(1)}, u32[]{:S(2)}, u32[]{:S(2)}) collective-permute-start(f32[4,4,1,1024]{3,2,1,0:T(1,128)S(1)} %get-tuple-element.182), channel_id=1, source_target_pairs={{256,0},{257,1},{258,2},{259,3},{260,4},{261,5},{262,6},{263,7},{2... | collective-permute-start | bytes 196616 | tf_op jit(solution)/shard_map/ppermute | solution.py:20
  112.5 6.9 %collective-permute-start.21 = (f32[1,4,10,1024]{3,2,1,0:T(8,128)S(1)}, f32[1,4,10,1024]{3,2,1,0:T(8,128)S(1)}, u32[]{:S(2)}, u32[]{:S(2)}) collective-permute-start(f32[1,4,10,1024]{3,2,1,0:T(8,128)S(1)} %get-tuple-element.173), channel_id=1, source_target_pairs={{0,32},{32,64},{64,96},{96,128},{128,160},{160,192},{192,224},{1,3... | collective-permute-start | bytes 491528 | tf_op jit(solution)/shard_map/ppermute | solution.py:17
  116.1 8.3 %collective-permute-start.22 = (f32[1,4,10,1024]{3,2,1,0:T(8,128)S(1)}, f32[1,4,10,1024]{3,2,1,0:T(8,128)S(1)}, u32[]{:S(2)}, u32[]{:S(2)}) collective-permute-start(f32[1,4,10,1024]{3,2,1,0:T(8,128)S(1)} %get-tuple-element.174), channel_id=1, source_target_pairs={{32,0},{64,32},{96,64},{128,96},{160,128},{192,160},{224,192},{33,... | collective-permute-start | bytes 491528 | tf_op jit(solution)/shard_map/ppermute | solution.py:20
  125.4 11.6 %collective-permute-start.23 = (f32[6,1,10,1024]{3,2,1,0:T(8,128)}, f32[6,1,10,1024]{3,2,1,0:T(8,128)}, u32[]{:S(2)}, u32[]{:S(2)}) collective-permute-start(f32[6,1,10,1024]{3,2,1,0:T(8,128)} %get-tuple-element.165), channel_id=1, source_target_pairs={{0,1},{1,2},{2,3},{3,4},{4,5},{5,6},{6,7},{7,8},{8,9},{9,10},{10,1... | collective-permute-start | bytes 737288 | tf_op jit(solution)/shard_map/ppermute | solution.py:17
  132.0 9.4 %collective-permute-start.24 = (f32[6,1,10,1024]{3,2,1,0:T(8,128)}, f32[6,1,10,1024]{3,2,1,0:T(8,128)}, u32[]{:S(2)}, u32[]{:S(2)}) collective-permute-start(f32[6,1,10,1024]{3,2,1,0:T(8,128)} %get-tuple-element.166), channel_id=1, source_target_pairs={{1,0},{2,1},{3,2},{4,3},{5,4},{6,5},{7,6},{8,7},{9,8},{10,9},{11,1... | collective-permute-start | bytes 737288 | tf_op jit(solution)/shard_map/ppermute | solution.py:20
  144.5 144.8 %copy-start.1 = (f32[8]{0:T(128)S(1)}, f32[8]{0:T(128)}, u32[]{:S(2)}) copy-start(f32[8]{0:T(128)} %param.7) | copy-start | bytes 100
Sparse Core Ops, SparseCore 0:
  290.4 40.2 all-reduce.7
where the time goes:
time: 340 us
  other arithmetic  150 us (44%)
  waiting for transfers between devices  81.1 us (24%)
  starting transfers between devices  76.5 us (22%)
  between operations  14.6 us (4%)
  loops' own time  6.9 us (2%)
  blocking collectives  5.96 us (2%)
  local copies, waits for them, and re-layouts  4.75 us (1%)
    reduce_sum x128, other arithmetic, add_block(): return total + jnp.sum(piece[:, :, None] * weights, axis=1)  135 us
    ppermute x12, starting transfers between devices, extended(): lax.ppermute(lax.slice_in_dim(block, block.shape[dim] - width, None, axis...  55.1 us
    psum x1, waiting for transfers between devices, shards(): lax.psum((partial_stack, jnp.sum(offset_weight)), 'off')  33.8 us
    ppermute x12, waiting for transfers between devices, extended(): lax.ppermute(lax.slice_in_dim(block, 0, width, axis=dim), axis, backward)  33 us
    ppermute x12, starting transfers between devices, extended(): lax.ppermute(lax.slice_in_dim(block, 0, width, axis=dim), axis, backward)  20.1 us
    ppermute x12, waiting for transfers between devices, extended(): lax.ppermute(lax.slice_in_dim(block, block.shape[dim] - width, None, axis...  10.2 us
  transfers between devices with their start and end apart: 26, of which 15 were waited for; matrix products, arithmetic and copies ran while one was open for 1% of the time, Pallas kernels for 0%

commit v1 on v0

--- a/solution.py
+++ b/solution.py
@@ -1,6 +1,8 @@
 import jax
 import jax.numpy as jnp
 from jax import lax
+from jax.experimental import pallas as pl
+from jax.experimental.pallas import tpu as pltpu
 from jax.sharding import PartitionSpec as P
 
 ITERS = 3
@@ -55,21 +57,79 @@
     return 0.5 * (padded[..., 2:] - padded[..., :-2])
 
 
-def move_gather(item):
-    traces, places = item
-    samples = traces.shape[1]
-    block = min(samples, 128)
-    outputs = jnp.arange(samples, dtype=jnp.float32)
+T = 1024
+NA = 16
+NB = 64
+KC = 512
 
-    def add_block(turn, total):
-        start = turn * block
-        piece = lax.dynamic_slice_in_dim(traces, start, block, 1)
-        where = lax.dynamic_slice_in_dim(places, start, block, 1)
-        weights = jnp.maximum(0.0, 1.0 - jnp.abs(where[:, :, None] - outputs[None, None, :]))
-        return total + jnp.sum(piece[:, :, None] * weights, axis=1)
 
-    empty = jnp.zeros(traces.shape, jnp.float32)
-    return lax.fori_loop(0, samples // block, add_block, empty)
+def moveout_kernel(first_ref, w_ref, data_ref, slope_ref, out_ref):
+    tt = lax.broadcasted_iota(jnp.int32, (8, T), 1).astype(jnp.float32) + 1.0
+    hh = lax.broadcasted_iota(jnp.int32, (8, T), 0).astype(jnp.float32) + (0.5 + first_ref[0])
+    tth = tt * hh
+    ttq = tt * tt
+    w = w_ref[...]
+    rows = lax.broadcasted_iota(jnp.int32, (NA, 128), 0)
+    rows = jnp.where(rows < 8, 2 * rows, 2 * rows - 15)
+    ia = rows.astype(jnp.float32).astype(jnp.bfloat16)
+    ib = lax.broadcasted_iota(jnp.int32, (NB, 128), 0).astype(jnp.float32).astype(jnp.bfloat16)
+    zero = jnp.zeros((NA, 128), jnp.bfloat16)
+    one_b = jnp.ones((NB, 128), jnp.bfloat16)
+    zero_b = jnp.zeros((NB, 128), jnp.bfloat16)
+    lane = lax.broadcasted_iota(jnp.int32, (8, 128), 1)
+    row = lax.broadcasted_iota(jnp.int32, (8, 128), 0)
+
+    def midpoint(m, carry):
+        s = slope_ref[m]
+        place = jnp.sqrt(jnp.maximum(ttq - tth * s, 1.0)) - 1.0
+        low = jnp.floor(place)
+        f = place - low
+        idx = jnp.minimum(low, float(T))
+        a = jnp.floor(idx * (1.0 / NB))
+        b = idx - a * NB
+        v = data_ref[m] * w
+        x1 = v * f
+        x0 = v - x1
+        x0h = x0.astype(jnp.bfloat16).astype(jnp.float32)
+        x1h = x1.astype(jnp.bfloat16).astype(jnp.float32)
+        values = (x0h, x0 - x0h, x1h, x1 - x1h)
+        acc = jnp.zeros((4 * NA, NB), jnp.float32)
+        for h in range(8):
+            for c in range(0, T, KC):
+                left, right = [], []
+                for l in range(c, c + KC, 128):
+                    def spread(x, n):
+                        part = x[h:h + 1, l:l + 128]
+                        return jnp.broadcast_to(part, (n, 128)).astype(jnp.bfloat16)
+                    hit = spread(a, NA) == ia
+                    left.append(jnp.concatenate(
+                        [jnp.where(hit, spread(x, NA), zero) for x in values], axis=0))
+                    right.append(jnp.where(spread(b, NB) == ib, one_b, zero_b))
+                acc = acc + lax.dot_general(
+                    jnp.concatenate(left, axis=1), jnp.concatenate(right, axis=1),
+                    (((1,), (1,)), ((), ())), preferred_element_type=jnp.float32)
+        lower = acc[:NA] + acc[NA:2 * NA]
+        upper = acc[2 * NA:3 * NA] + acc[3 * NA:]
+        lower = jnp.concatenate([lower[:8], lower[8:]], axis=1)
+        upper = jnp.concatenate([upper[:8], upper[8:]], axis=1)
+        upper = pltpu.roll(upper, 1, 1)
+        before = pltpu.roll(upper, 1, 0)
+        upper = jnp.where(lane == 0, jnp.where(row == 0, 0.0, before), upper)
+        out_ref[m] = lower + upper
+        return carry
+
+    lax.fori_loop(0, 16, midpoint, 0)
+
+
+def moveout(first, w, data, slope):
+    return pl.pallas_call(
+        moveout_kernel,
+        out_shape=jax.ShapeDtypeStruct((16, 8, 128), jnp.float32),
+        in_specs=[pl.BlockSpec(memory_space=pltpu.SMEM)]
+        + [pl.BlockSpec(memory_space=pltpu.VMEM)] * 3,
+        out_specs=pl.BlockSpec(memory_space=pltpu.VMEM),
+        name="moveout",
+    )(first, w, data, slope)
 
 
 def shards(data, offset_weight):
@@ -84,17 +144,13 @@
     for step in range(ITERS):
         slope = slope - smooth(gradient * (residual + slope * gradient)) / denominator
     first_offset = (lax.axis_index("off") * local_offsets).astype(jnp.float32)
-    times = jnp.arange(samples, dtype=jnp.float32) + 1.0
-    offsets = jnp.arange(local_offsets, dtype=jnp.float32) + 0.5 + first_offset
-    squared = times * times - times * offsets[:, None] * slope
-    target = jnp.sqrt(jnp.maximum(squared, 1.0)) - 1.0
-    midpoints = data.shape[0] * data.shape[1]
-    traces = data.reshape(midpoints, local_offsets, samples)
-    places = target.reshape(midpoints, local_offsets, samples)
-    corrected = lax.map(move_gather, (traces, places)).reshape(data.shape)
-    partial_stack = jnp.sum(corrected * offset_weight[None, None, :, None], axis=2)
-    stack_total, weight_sum = lax.psum((partial_stack, jnp.sum(offset_weight)), "off")
-    stacked = stack_total / weight_sum
+    partial = moveout(
+        first_offset.reshape(1), offset_weight.reshape(8, 1),
+        data.reshape(16, 8, T), slope.reshape(16, 8, T))
+    packed = jnp.concatenate(
+        [partial.reshape(4, 4, T), jnp.full((4, 4, 128), jnp.sum(offset_weight))], axis=2)
+    total = packed + lax.ppermute(packed, "off", [(0, 1), (1, 0)])
+    stacked = total[:, :, :T] / total[:, :, T:T + 1]
     return (slope, stacked)
 
 

time: 340 us -> 168 us (0.49)
  the two profiles are of different devices: /device:TPU:1 before, /device:TPU:46 now
where the time goes in v1:
time: 168 us; the launch traced here: 167 us
  starting transfers between devices  80.2 us (48%)
  waiting for transfers between devices  56.7 us (34%)
  Pallas kernels  13.4 us (8%)
  other arithmetic  10.8 us (6%)
  local copies, waits for them, and re-layouts  4.83 us (3%)
    ppermute x12, starting transfers between devices, extended(): lax.ppermute(lax.slice_in_dim(block, 0, width, axis=dim), axis, backward)  50.8 us
    ppermute x12, waiting for transfers between devices, extended(): lax.ppermute(lax.slice_in_dim(block, block.shape[dim] - width, None, axis...  38.9 us
    ppermute x12, starting transfers between devices, extended(): lax.ppermute(lax.slice_in_dim(block, block.shape[dim] - width, None, axis...  24.2 us
    pallas_call x1, Pallas kernels, moveout(): pl.pallas_call(moveout_kernel, out_shape=jax.ShapeDtypeStruct((16, 8, 128...  13.4 us
    ppermute x12, waiting for transfers between devices, extended(): lax.ppermute(lax.slice_in_dim(block, 0, width, axis=dim), axis, backward)  11.2 us
    ppermute x1, waiting for transfers between devices, shards(): total = packed + lax.ppermute(packed, 'off', [(0, 1), (1, 0)])  5.82 us
    add x12, other arithmetic, weighted_box(): return 0.25 * left + 0.5 * middle + 0.25 * right  3.44 us
  transfers between devices with their start and end apart: 26, of which 18 were waited for; matrix products, arithmetic and copies ran while one was open for 2% of the time, Pallas kernels for 0%

profile of v1, /device:TPU:46, one launch (start us, length us, event | category | flops | bytes accessed | tf_op | source)
XLA Modules:
  0.0 167.1 jit_solution(6449828513456455424)
XLA Ops:
  1.8 3.3 %collective-permute-start = (f32[4,4,1,1024]{3,2,1,0:T(1,128)S(1)}, f32[4,4,1,1024]{3,2,1,0:T(1,128)S(1)}, u32[]{:S(2)}, u32[]{:S(2)}) collective-permute-start(f32[4,4,1,1024]{3,2,1,0:T(1,128)S(1)} %slice.235), channel_id=1, source_target_pairs={{256,0},{257,1},{258,2},{259,3},{260,4},{261,5},{262,6},{263,7},{2... | collective-permute-start | bytes 196616 | tf_op jit(solution)/shard_map/ppermute | solution.py:30
  8.2 5.8 %collective-permute-start.2 = (f32[4,4,1,1024]{3,2,1,0:T(1,128)S(1)}, f32[4,4,1,1024]{3,2,1,0:T(1,128)S(1)}, u32[]{:S(2)}, u32[]{:S(2)}) collective-permute-start(f32[4,4,1,1024]{3,2,1,0:T(1,128)S(1)} %get-tuple-element.32), channel_id=1, source_target_pairs={{256,0},{257,1},{258,2},{259,3},{260,4},{261,5},{262,6},{263,7},{2... | collective-permute-start | bytes 196616 | tf_op jit(solution)/shard_map/ppermute | solution.py:22
  15.7 6.1 %collective-permute-start.8 = (f32[4,4,1,1024]{3,2,1,0:T(1,128)S(1)}, f32[4,4,1,1024]{3,2,1,0:T(1,128)S(1)}, u32[]{:S(2)}, u32[]{:S(2)}) collective-permute-start(f32[4,4,1,1024]{3,2,1,0:T(1,128)S(1)} %get-tuple-element.30), channel_id=1, source_target_pairs={{256,0},{257,1},{258,2},{259,3},{260,4},{261,5},{262,6},{263,7},{2... | collective-permute-start | bytes 196616 | tf_op jit(solution)/shard_map/ppermute | solution.py:22
  23.2 3.3 %collective-permute-start.4 = (f32[1,4,10,1024]{3,2,1,0:T(8,128)S(1)}, f32[1,4,10,1024]{3,2,1,0:T(8,128)S(1)}, u32[]{:S(2)}, u32[]{:S(2)}) collective-permute-start(f32[1,4,10,1024]{3,2,1,0:T(8,128)S(1)} %get-tuple-element.24), channel_id=1, source_target_pairs={{32,0},{64,32},{96,64},{128,96},{160,128},{192,160},{224,192},{33,... | collective-permute-start | bytes 491528 | tf_op jit(solution)/shard_map/ppermute | solution.py:22
  26.4 2.6 %collective-permute-start.3 = (f32[1,4,10,1024]{3,2,1,0:T(8,128)S(1)}, f32[1,4,10,1024]{3,2,1,0:T(8,128)S(1)}, u32[]{:S(2)}, u32[]{:S(2)}) collective-permute-start(f32[1,4,10,1024]{3,2,1,0:T(8,128)S(1)} %get-tuple-element.23), channel_id=1, source_target_pairs={{0,32},{32,64},{64,96},{96,128},{128,160},{160,192},{192,224},{1,3... | collective-permute-start | bytes 491528 | tf_op jit(solution)/shard_map/ppermute | solution.py:19
  29.5 3.3 %collective-permute-start.10 = (f32[1,4,10,1024]{3,2,1,0:T(8,128)S(1)}, f32[1,4,10,1024]{3,2,1,0:T(8,128)S(1)}, u32[]{:S(2)}, u32[]{:S(2)}) collective-permute-start(f32[1,4,10,1024]{3,2,1,0:T(8,128)S(1)} %get-tuple-element.22), channel_id=1, source_target_pairs={{32,0},{64,32},{96,64},{128,96},{160,128},{192,160},{224,192},{33,... | collective-permute-start | bytes 491528 | tf_op jit(solution)/shard_map/ppermute | solution.py:22
  32.8 2.6 %collective-permute-start.9 = (f32[1,4,10,1024]{3,2,1,0:T(8,128)S(1)}, f32[1,4,10,1024]{3,2,1,0:T(8,128)S(1)}, u32[]{:S(2)}, u32[]{:S(2)}) collective-permute-start(f32[1,4,10,1024]{3,2,1,0:T(8,128)S(1)} %get-tuple-element.21), channel_id=1, source_target_pairs={{0,32},{32,64},{64,96},{96,128},{128,160},{160,192},{192,224},{1,3... | collective-permute-start | bytes 491528 | tf_op jit(solution)/shard_map/ppermute | solution.py:19
  35.5 6.3 %collective-permute-start.6 = (f32[6,1,10,1024]{3,2,1,0:T(8,128)S(1)}, f32[6,1,10,1024]{3,2,1,0:T(8,128)S(1)}, u32[]{:S(2)}, u32[]{:S(2)}) collective-permute-start(f32[6,1,10,1024]{3,2,1,0:T(8,128)S(1)} %get-tuple-element.16), channel_id=1, source_target_pairs={{1,0},{2,1},{3,2},{4,3},{5,4},{6,5},{7,6},{8,7},{9,8},{10,9},{11,1... | collective-permute-start | bytes 737288 | tf_op jit(solution)/shard_map/ppermute | solution.py:22
  41.8 1.9 %collective-permute-start.5 = (f32[6,1,10,1024]{3,2,1,0:T(8,128)S(1)}, f32[6,1,10,1024]{3,2,1,0:T(8,128)S(1)}, u32[]{:S(2)}, u32[]{:S(2)}) collective-permute-start(f32[6,1,10,1024]{3,2,1,0:T(8,128)S(1)} %get-tuple-element.15), channel_id=1, source_target_pairs={{0,1},{1,2},{2,3},{3,4},{4,5},{5,6},{6,7},{7,8},{8,9},{9,10},{10,1... | collective-permute-start | bytes 737288 | tf_op jit(solution)/shard_map/ppermute | solution.py:19
  43.9 6.1 %collective-permute-start.12 = (f32[6,1,10,1024]{3,2,1,0:T(8,128)S(1)}, f32[6,1,10,1024]{3,2,1,0:T(8,128)S(1)}, u32[]{:S(2)}, u32[]{:S(2)}) collective-permute-start(f32[6,1,10,1024]{3,2,1,0:T(8,128)S(1)} %get-tuple-element.14), channel_id=1, source_target_pairs={{1,0},{2,1},{3,2},{4,3},{5,4},{6,5},{7,6},{8,7},{9,8},{10,9},{11,1... | collective-permute-start | bytes 737288 | tf_op jit(solution)/shard_map/ppermute | solution.py:22
  50.0 1.9 %collective-permute-start.11 = (f32[6,1,10,1024]{3,2,1,0:T(8,128)S(1)}, f32[6,1,10,1024]{3,2,1,0:T(8,128)S(1)}, u32[]{:S(2)}, u32[]{:S(2)}) collective-permute-start(f32[6,1,10,1024]{3,2,1,0:T(8,128)S(1)} %get-tuple-element.13), channel_id=1, source_target_pairs={{0,1},{1,2},{2,3},{3,4},{4,5},{5,6},{6,7},{7,8},{8,9},{9,10},{10,1... | collective-permute-start | bytes 737288 | tf_op jit(solution)/shard_map/ppermute | solution.py:19
  55.2 6.0 %collective-permute-done.11 = f32[6,1,10,1024]{3,2,1,0:T(8,128)S(1)} collective-permute-done((f32[6,1,10,1024]{3,2,1,0:T(8,128)S(1)}, f32[6,1,10,1024]{3,2,1,0:T(8,128)S(1)}, u32[]{:S(2)}, u32[]{:S(2)}) %collective-permute-start.11) | collective-permute-done | bytes 245792 | tf_op jit(solution)/shard_map/ppermute | solution.py:19
  62.9 6.9 %collective-permute-start.14 = (f32[4,4,1,1024]{3,2,1,0:T(1,128)S(1)}, f32[4,4,1,1024]{3,2,1,0:T(1,128)S(1)}, u32[]{:S(2)}, u32[]{:S(2)}) collective-permute-start(f32[4,4,1,1024]{3,2,1,0:T(1,128)S(1)} %get-tuple-element.28), channel_id=1, source_target_pairs={{256,0},{257,1},{258,2},{259,3},{260,4},{261,5},{262,6},{263,7},{2... | collective-permute-start | bytes 196616 | tf_op jit(solution)/shard_map/ppermute | solution.py:22
  71.8 5.8 %collective-permute-done.13 = f32[4,4,1,1024]{3,2,1,0:T(1,128)S(1)} collective-permute-done((f32[4,4,1,1024]{3,2,1,0:T(1,128)S(1)}, f32[4,4,1,1024]{3,2,1,0:T(1,128)S(1)}, u32[]{:S(2)}, u32[]{:S(2)}) %collective-permute-start.13) | collective-permute-done | bytes 65568 | tf_op jit(solution)/shard_map/ppermute | solution.py:19
  77.6 2.6 %collective-permute-start.16 = (f32[1,4,10,1024]{3,2,1,0:T(8,128)S(1)}, f32[1,4,10,1024]{3,2,1,0:T(8,128)S(1)}, u32[]{:S(2)}, u32[]{:S(2)}) collective-permute-start(f32[1,4,10,1024]{3,2,1,0:T(8,128)S(1)} %get-tuple-element.20), channel_id=1, source_target_pairs={{32,0},{64,32},{96,64},{128,96},{160,128},{192,160},{224,192},{33,... | collective-permute-start | bytes 491528 | tf_op jit(solution)/shard_map/ppermute | solution.py:22
  80.2 3.3 %collective-permute-start.15 = (f32[1,4,10,1024]{3,2,1,0:T(8,128)S(1)}, f32[1,4,10,1024]{3,2,1,0:T(8,128)S(1)}, u32[]{:S(2)}, u32[]{:S(2)}) collective-permute-start(f32[1,4,10,1024]{3,2,1,0:T(8,128)S(1)} %get-tuple-element.19), channel_id=1, source_target_pairs={{0,32},{32,64},{64,96},{96,128},{128,160},{160,192},{192,224},{1,3... | collective-permute-start | bytes 491528 | tf_op jit(solution)/shard_map/ppermute | solution.py:19
  83.5 2.4 %collective-permute-done.16 = f32[1,4,10,1024]{3,2,1,0:T(8,128)S(1)} collective-permute-done((f32[1,4,10,1024]{3,2,1,0:T(8,128)S(1)}, f32[1,4,10,1024]{3,2,1,0:T(8,128)S(1)}, u32[]{:S(2)}, u32[]{:S(2)}) %collective-permute-start.16) | collective-permute-done | bytes 163872 | tf_op jit(solution)/shard_map/ppermute | solution.py:22
  85.9 3.5 %collective-permute-done.15 = f32[1,4,10,1024]{3,2,1,0:T(8,128)S(1)} collective-permute-done((f32[1,4,10,1024]{3,2,1,0:T(8,128)S(1)}, f32[1,4,10,1024]{3,2,1,0:T(8,128)S(1)}, u32[]{:S(2)}, u32[]{:S(2)}) %collective-permute-start.15) | collective-permute-done | bytes 163872 | tf_op jit(solution)/shard_map/ppermute | solution.py:19
  89.5 1.9 %collective-permute-start.18 = (f32[6,1,10,1024]{3,2,1,0:T(8,128)S(1)}, f32[6,1,10,1024]{3,2,1,0:T(8,128)S(1)}, u32[]{:S(2)}, u32[]{:S(2)}) collective-permute-start(f32[6,1,10,1024]{3,2,1,0:T(8,128)S(1)} %get-tuple-element.12), channel_id=1, source_target_pairs={{1,0},{2,1},{3,2},{4,3},{5,4},{6,5},{7,6},{8,7},{9,8},{10,9},{11,1... | collective-permute-start | bytes 737288 | tf_op jit(solution)/shard_map/ppermute | solution.py:22
  91.4 2.4 %collective-permute-start.17 = (f32[6,1,10,1024]{3,2,1,0:T(8,128)S(1)}, f32[6,1,10,1024]{3,2,1,0:T(8,128)S(1)}, u32[]{:S(2)}, u32[]{:S(2)}) collective-permute-start(f32[6,1,10,1024]{3,2,1,0:T(8,128)S(1)} %get-tuple-element.11), channel_id=1, source_target_pairs={{0,1},{1,2},{2,3},{3,4},{4,5},{5,6},{6,7},{7,8},{8,9},{9,10},{10,1... | collective-permute-start | bytes 737288 | tf_op jit(solution)/shard_map/ppermute | solution.py:19
  93.8 2.9 %collective-permute-done.18 = f32[6,1,10,1024]{3,2,1,0:T(8,128)S(1)} collective-permute-done((f32[6,1,10,1024]{3,2,1,0:T(8,128)S(1)}, f32[6,1,10,1024]{3,2,1,0:T(8,128)S(1)}, u32[]{:S(2)}, u32[]{:S(2)}) %collective-permute-start.18) | collective-permute-done | bytes 245792 | tf_op jit(solution)/shard_map/ppermute | solution.py:22
  96.7 5.9 %collective-permute-done.17 = f32[6,1,10,1024]{3,2,1,0:T(8,128)S(1)} collective-permute-done((f32[6,1,10,1024]{3,2,1,0:T(8,128)S(1)}, f32[6,1,10,1024]{3,2,1,0:T(8,128)S(1)}, u32[]{:S(2)}, u32[]{:S(2)}) %collective-permute-start.17) | collective-permute-done | bytes 245792 | tf_op jit(solution)/shard_map/ppermute | solution.py:19
  107.8 5.8 %collective-permute-done.19 = f32[4,4,1,1024]{3,2,1,0:T(1,128)S(1)} collective-permute-done((f32[4,4,1,1024]{3,2,1,0:T(1,128)S(1)}, f32[4,4,1,1024]{3,2,1,0:T(1,128)S(1)}, u32[]{:S(2)}, u32[]{:S(2)}) %collective-permute-start.19) | collective-permute-done | bytes 65568 | tf_op jit(solution)/shard_map/ppermute | solution.py:19
  113.7 5.1 %collective-permute-start.22 = (f32[1,4,10,1024]{3,2,1,0:T(8,128)S(1)}, f32[1,4,10,1024]{3,2,1,0:T(8,128)S(1)}, u32[]{:S(2)}, u32[]{:S(2)}) collective-permute-start(f32[1,4,10,1024]{3,2,1,0:T(8,128)S(1)} %get-tuple-element.18), channel_id=1, source_target_pairs={{32,0},{64,32},{96,64},{128,96},{160,128},{192,160},{224,192},{33,... | collective-permute-start | bytes 491528 | tf_op jit(solution)/shard_map/ppermute | solution.py:22
  118.9 1.9 %collective-permute-start.21 = (f32[1,4,10,1024]{3,2,1,0:T(8,128)S(1)}, f32[1,4,10,1024]{3,2,1,0:T(8,128)S(1)}, u32[]{:S(2)}, u32[]{:S(2)}) collective-permute-start(f32[1,4,10,1024]{3,2,1,0:T(8,128)S(1)} %get-tuple-element.17), channel_id=1, source_target_pairs={{0,32},{32,64},{64,96},{96,128},{128,160},{160,192},{192,224},{1,3... | collective-permute-start | bytes 491528 | tf_op jit(solution)/shard_map/ppermute | solution.py:19
  120.8 1.9 %collective-permute-done.22 = f32[1,4,10,1024]{3,2,1,0:T(8,128)S(1)} collective-permute-done((f32[1,4,10,1024]{3,2,1,0:T(8,128)S(1)}, f32[1,4,10,1024]{3,2,1,0:T(8,128)S(1)}, u32[]{:S(2)}, u32[]{:S(2)}) %collective-permute-start.22) | collective-permute-done | bytes 163872 | tf_op jit(solution)/shard_map/ppermute | solution.py:22
  122.7 4.4 %collective-permute-done.21 = f32[1,4,10,1024]{3,2,1,0:T(8,128)S(1)} collective-permute-done((f32[1,4,10,1024]{3,2,1,0:T(8,128)S(1)}, f32[1,4,10,1024]{3,2,1,0:T(8,128)S(1)}, u32[]{:S(2)}, u32[]{:S(2)}) %collective-permute-start.21) | collective-permute-done | bytes 163872 | tf_op jit(solution)/shard_map/ppermute | solution.py:19
  129.9 2.4 %collective-permute-start.23 = (f32[6,1,10,1024]{3,2,1,0:T(8,128)S(1)}, f32[6,1,10,1024]{3,2,1,0:T(8,128)S(1)}, u32[]{:S(2)}, u32[]{:S(2)}) collective-permute-start(f32[6,1,10,1024]{3,2,1,0:T(8,128)S(1)} %get-tuple-element.9), channel_id=1, source_target_pairs={{0,1},{1,2},{2,3},{3,4},{4,5},{5,6},{6,7},{7,8},{8,9},{9,10},{10,1... | collective-permute-start | bytes 737288 | tf_op jit(solution)/shard_map/ppermute | solution.py:19
  135.5 5.7 %collective-permute-done.23 = f32[6,1,10,1024]{3,2,1,0:T(8,128)S(1)} collective-permute-done((f32[6,1,10,1024]{3,2,1,0:T(8,128)S(1)}, f32[6,1,10,1024]{3,2,1,0:T(8,128)S(1)}, u32[]{:S(2)}, u32[]{:S(2)}) %collective-permute-start.23) | collective-permute-done | bytes 245792 | tf_op jit(solution)/shard_map/ppermute | solution.py:19
  143.0 13.4 %moveout.1 = f32[16,8,128]{2,1,0:T(8,128)} custom-call(f32[1]{0:T(128)} %bitcast.first_ref, f32[8,1]{1,0:T(8,128)} %copy.5.w_ref, f32[16,8,1024]{2,1,0:T(8,128)} %bitcast.4, f32[16,8,1024]{2,1,0:T(8,128)} %bitcast.5), custom_call_target="tpu_custom_call" | custom-call | tf_op jit(solution)/shard_map/moveout/pallas_call | solution.py:125
  157.9 1.9 %collective-permute-start.25 = (f32[4,4,1152]{2,1,0:T(4,128)S(1)}, f32[4,4,1152]{2,1,0:T(4,128)S(1)}, u32[]{:S(2)}, u32[]{:S(2)}) collective-permute-start(f32[4,4,1152]{2,1,0:T(4,128)S(1)} %concatenate.55), channel_id=1, source_target_pairs={{0,256},{256,0},{1,257},{257,1},{2,258},{258,2},{3,259},{259,3},{4... | collective-permute-start | bytes 221192 | tf_op jit(solution)/shard_map/ppermute | solution.py:152
  159.8 5.8 %collective-permute-done.25 = f32[4,4,1152]{2,1,0:T(4,128)S(1)} collective-permute-done((f32[4,4,1152]{2,1,0:T(4,128)S(1)}, f32[4,4,1152]{2,1,0:T(4,128)S(1)}, u32[]{:S(2)}, u32[]{:S(2)}) %collective-permute-start.25) | collective-permute-done | bytes 73760 | tf_op jit(solution)/shard_map/ppermute | solution.py:152
  (67 shorter events, 31.0 us)
Async XLA Ops:
  0.6 6.5 %copy-start = (f32[4,4,8,1024]{3,2,1,0:T(8,128)S(1)}, f32[4,4,8,1024]{3,2,1,0:T(8,128)}, u32[]{:S(2)}) copy-start(f32[4,4,8,1024]{3,2,1,0:T(8,128)} %param.2) | copy-start | bytes 1572868
  1.8 5.2 %collective-permute-start = (f32[4,4,1,1024]{3,2,1,0:T(1,128)S(1)}, f32[4,4,1,1024]{3,2,1,0:T(1,128)S(1)}, u32[]{:S(2)}, u32[]{:S(2)}) collective-permute-start(f32[4,4,1,1024]{3,2,1,0:T(1,128)S(1)} %slice.235), channel_id=1, source_target_pairs={{256,0},{257,1},{258,2},{259,3},{260,4},{261,5},{262,6},{263,7},{2... | collective-permute-start | bytes 196616 | tf_op jit(solution)/shard_map/ppermute | solution.py:30
  8.2 14.9 %collective-permute-start.2 = (f32[4,4,1,1024]{3,2,1,0:T(1,128)S(1)}, f32[4,4,1,1024]{3,2,1,0:T(1,128)S(1)}, u32[]{:S(2)}, u32[]{:S(2)}) collective-permute-start(f32[4,4,1,1024]{3,2,1,0:T(1,128)S(1)} %get-tuple-element.32), channel_id=1, source_target_pairs={{256,0},{257,1},{258,2},{259,3},{260,4},{261,5},{262,6},{263,7},{2... | collective-permute-start | bytes 196616 | tf_op jit(solution)/shard_map/ppermute | solution.py:22
  14.0 9.1 %collective-permute-start.1 = (f32[4,4,1,1024]{3,2,1,0:T(1,128)S(1)}, f32[4,4,1,1024]{3,2,1,0:T(1,128)S(1)}, u32[]{:S(2)}, u32[]{:S(2)}) collective-permute-start(f32[4,4,1,1024]{3,2,1,0:T(1,128)S(1)} %get-tuple-element.31), channel_id=1, source_target_pairs={{0,256},{1,257},{2,258},{3,259},{4,260},{5,261},{6,262},{7,263},{8... | collective-permute-start | bytes 196616 | tf_op jit(solution)/shard_map/ppermute | solution.py:19
  15.7 13.3 %collective-permute-start.8 = (f32[4,4,1,1024]{3,2,1,0:T(1,128)S(1)}, f32[4,4,1,1024]{3,2,1,0:T(1,128)S(1)}, u32[]{:S(2)}, u32[]{:S(2)}) collective-permute-start(f32[4,4,1,1024]{3,2,1,0:T(1,128)S(1)} %get-tuple-element.30), channel_id=1, source_target_pairs={{256,0},{257,1},{258,2},{259,3},{260,4},{261,5},{262,6},{263,7},{2... | collective-permute-start | bytes 196616 | tf_op jit(solution)/shard_map/ppermute | solution.py:22
  21.8 7.7 %collective-permute-start.7 = (f32[4,4,1,1024]{3,2,1,0:T(1,128)S(1)}, f32[4,4,1,1024]{3,2,1,0:T(1,128)S(1)}, u32[]{:S(2)}, u32[]{:S(2)}) collective-permute-start(f32[4,4,1,1024]{3,2,1,0:T(1,128)S(1)} %get-tuple-element.29), channel_id=1, source_target_pairs={{0,256},{1,257},{2,258},{3,259},{4,260},{5,261},{6,262},{7,263},{8... | collective-permute-start | bytes 196616 | tf_op jit(solution)/shard_map/ppermute | solution.py:19
  23.2 12.2 %collective-permute-start.4 = (f32[1,4,10,1024]{3,2,1,0:T(8,128)S(1)}, f32[1,4,10,1024]{3,2,1,0:T(8,128)S(1)}, u32[]{:S(2)}, u32[]{:S(2)}) collective-permute-start(f32[1,4,10,1024]{3,2,1,0:T(8,128)S(1)} %get-tuple-element.24), channel_id=1, source_target_pairs={{32,0},{64,32},{96,64},{128,96},{160,128},{192,160},{224,192},{33,... | collective-permute-start | bytes 491528 | tf_op jit(solution)/shard_map/ppermute | solution.py:22
  26.4 9.0 %collective-permute-start.3 = (f32[1,4,10,1024]{3,2,1,0:T(8,128)S(1)}, f32[1,4,10,1024]{3,2,1,0:T(8,128)S(1)}, u32[]{:S(2)}, u32[]{:S(2)}) collective-permute-start(f32[1,4,10,1024]{3,2,1,0:T(8,128)S(1)} %get-tuple-element.23), channel_id=1, source_target_pairs={{0,32},{32,64},{64,96},{96,128},{128,160},{160,192},{192,224},{1,3... | collective-permute-start | bytes 491528 | tf_op jit(solution)/shard_map/ppermute | solution.py:19
  29.5 14.2 %collective-permute-start.10 = (f32[1,4,10,1024]{3,2,1,0:T(8,128)S(1)}, f32[1,4,10,1024]{3,2,1,0:T(8,128)S(1)}, u32[]{:S(2)}, u32[]{:S(2)}) collective-permute-start(f32[1,4,10,1024]{3,2,1,0:T(8,128)S(1)} %get-tuple-element.22), channel_id=1, source_target_pairs={{32,0},{64,32},{96,64},{128,96},{160,128},{192,160},{224,192},{33,... | collective-permute-start | bytes 491528 | tf_op jit(solution)/shard_map/ppermute | solution.py:22
  32.8 11.0 %collective-permute-start.9 = (f32[1,4,10,1024]{3,2,1,0:T(8,128)S(1)}, f32[1,4,10,1024]{3,2,1,0:T(8,128)S(1)}, u32[]{:S(2)}, u32[]{:S(2)}) collective-permute-start(f32[1,4,10,1024]{3,2,1,0:T(8,128)S(1)} %get-tuple-element.21), channel_id=1, source_target_pairs={{0,32},{32,64},{64,96},{96,128},{128,160},{160,192},{192,224},{1,3... | collective-permute-start | bytes 491528 | tf_op jit(solution)/shard_map/ppermute | solution.py:19
  35.5 16.4 %collective-permute-start.6 = (f32[6,1,10,1024]{3,2,1,0:T(8,128)S(1)}, f32[6,1,10,1024]{3,2,1,0:T(8,128)S(1)}, u32[]{:S(2)}, u32[]{:S(2)}) collective-permute-start(f32[6,1,10,1024]{3,2,1,0:T(8,128)S(1)} %get-tuple-element.16), channel_id=1, source_target_pairs={{1,0},{2,1},{3,2},{4,3},{5,4},{6,5},{7,6},{8,7},{9,8},{10,9},{11,1... | collective-permute-start | bytes 737288 | tf_op jit(solution)/shard_map/ppermute | solution.py:22
  41.8 11.5 %collective-permute-start.5 = (f32[6,1,10,1024]{3,2,1,0:T(8,128)S(1)}, f32[6,1,10,1024]{3,2,1,0:T(8,128)S(1)}, u32[]{:S(2)}, u32[]{:S(2)}) collective-permute-start(f32[6,1,10,1024]{3,2,1,0:T(8,128)S(1)} %get-tuple-element.15), channel_id=1, source_target_pairs={{0,1},{1,2},{2,3},{3,4},{4,5},{5,6},{6,7},{7,8},{8,9},{9,10},{10,1... | collective-permute-start | bytes 737288 | tf_op jit(solution)/shard_map/ppermute | solution.py:19
  43.9 11.4 %collective-permute-start.12 = (f32[6,1,10,1024]{3,2,1,0:T(8,128)S(1)}, f32[6,1,10,1024]{3,2,1,0:T(8,128)S(1)}, u32[]{:S(2)}, u32[]{:S(2)}) collective-permute-start(f32[6,1,10,1024]{3,2,1,0:T(8,128)S(1)} %get-tuple-element.14), channel_id=1, source_target_pairs={{1,0},{2,1},{3,2},{4,3},{5,4},{6,5},{7,6},{8,7},{9,8},{10,9},{11,1... | collective-permute-start | bytes 737288 | tf_op jit(solution)/shard_map/ppermute | solution.py:22
  50.0 11.3 %collective-permute-start.11 = (f32[6,1,10,1024]{3,2,1,0:T(8,128)S(1)}, f32[6,1,10,1024]{3,2,1,0:T(8,128)S(1)}, u32[]{:S(2)}, u32[]{:S(2)}) collective-permute-start(f32[6,1,10,1024]{3,2,1,0:T(8,128)S(1)} %get-tuple-element.13), channel_id=1, source_target_pairs={{0,1},{1,2},{2,3},{3,4},{4,5},{5,6},{6,7},{7,8},{8,9},{9,10},{10,1... | collective-permute-start | bytes 737288 | tf_op jit(solution)/shard_map/ppermute | solution.py:19
  62.9 8.8 %collective-permute-start.14 = (f32[4,4,1,1024]{3,2,1,0:T(1,128)S(1)}, f32[4,4,1,1024]{3,2,1,0:T(1,128)S(1)}, u32[]{:S(2)}, u32[]{:S(2)}) collective-permute-start(f32[4,4,1,1024]{3,2,1,0:T(1,128)S(1)} %get-tuple-element.28), channel_id=1, source_target_pairs={{256,0},{257,1},{258,2},{259,3},{260,4},{261,5},{262,6},{263,7},{2... | collective-permute-start | bytes 196616 | tf_op jit(solution)/shard_map/ppermute | solution.py:22
  69.9 7.7 %collective-permute-start.13 = (f32[4,4,1,1024]{3,2,1,0:T(1,128)S(1)}, f32[4,4,1,1024]{3,2,1,0:T(1,128)S(1)}, u32[]{:S(2)}, u32[]{:S(2)}) collective-permute-start(f32[4,4,1,1024]{3,2,1,0:T(1,128)S(1)} %get-tuple-element.27), channel_id=1, source_target_pairs={{0,256},{1,257},{2,258},{3,259},{4,260},{5,261},{6,262},{7,263},{8... | collective-permute-start | bytes 196616 | tf_op jit(solution)/shard_map/ppermute | solution.py:19
  77.6 8.3 %collective-permute-start.16 = (f32[1,4,10,1024]{3,2,1,0:T(8,128)S(1)}, f32[1,4,10,1024]{3,2,1,0:T(8,128)S(1)}, u32[]{:S(2)}, u32[]{:S(2)}) collective-permute-start(f32[1,4,10,1024]{3,2,1,0:T(8,128)S(1)} %get-tuple-element.20), channel_id=1, source_target_pairs={{32,0},{64,32},{96,64},{128,96},{160,128},{192,160},{224,192},{33,... | collective-permute-start | bytes 491528 | tf_op jit(solution)/shard_map/ppermute | solution.py:22
  80.2 9.1 %collective-permute-start.15 = (f32[1,4,10,1024]{3,2,1,0:T(8,128)S(1)}, f32[1,4,10,1024]{3,2,1,0:T(8,128)S(1)}, u32[]{:S(2)}, u32[]{:S(2)}) collective-permute-start(f32[1,4,10,1024]{3,2,1,0:T(8,128)S(1)} %get-tuple-element.19), channel_id=1, source_target_pairs={{0,32},{32,64},{64,96},{96,128},{128,160},{160,192},{192,224},{1,3... | collective-permute-start | bytes 491528 | tf_op jit(solution)/shard_map/ppermute | solution.py:19
  89.5 7.2 %collective-permute-start.18 = (f32[6,1,10,1024]{3,2,1,0:T(8,128)S(1)}, f32[6,1,10,1024]{3,2,1,0:T(8,128)S(1)}, u32[]{:S(2)}, u32[]{:S(2)}) collective-permute-start(f32[6,1,10,1024]{3,2,1,0:T(8,128)S(1)} %get-tuple-element.12), channel_id=1, source_target_pairs={{1,0},{2,1},{3,2},{4,3},{5,4},{6,5},{7,6},{8,7},{9,8},{10,9},{11,1... | collective-permute-start | bytes 737288 | tf_op jit(solution)/shard_map/ppermute | solution.py:22
  91.4 11.2 %collective-permute-start.17 = (f32[6,1,10,1024]{3,2,1,0:T(8,128)S(1)}, f32[6,1,10,1024]{3,2,1,0:T(8,128)S(1)}, u32[]{:S(2)}, u32[]{:S(2)}) collective-permute-start(f32[6,1,10,1024]{3,2,1,0:T(8,128)S(1)} %get-tuple-element.11), channel_id=1, source_target_pairs={{0,1},{1,2},{2,3},{3,4},{4,5},{5,6},{6,7},{7,8},{8,9},{9,10},{10,1... | collective-permute-start | bytes 737288 | tf_op jit(solution)/shard_map/ppermute | solution.py:19
  103.8 28.5 %copy-start.1 = (f32[8]{0:T(128)S(1)}, f32[8]{0:T(128)}, u32[]{:S(2)}) copy-start(f32[8]{0:T(128)} %param.3) | copy-start | bytes 100
  104.3 3.6 %collective-permute-start.20 = (f32[4,4,1,1024]{3,2,1,0:T(1,128)S(1)}, f32[4,4,1,1024]{3,2,1,0:T(1,128)S(1)}, u32[]{:S(2)}, u32[]{:S(2)}) collective-permute-start(f32[4,4,1,1024]{3,2,1,0:T(1,128)S(1)} %get-tuple-element.26), channel_id=1, source_target_pairs={{256,0},{257,1},{258,2},{259,3},{260,4},{261,5},{262,6},{263,7},{2... | collective-permute-start | bytes 196616 | tf_op jit(solution)/shard_map/ppermute | solution.py:22
  106.0 7.7 %collective-permute-start.19 = (f32[4,4,1,1024]{3,2,1,0:T(1,128)S(1)}, f32[4,4,1,1024]{3,2,1,0:T(1,128)S(1)}, u32[]{:S(2)}, u32[]{:S(2)}) collective-permute-start(f32[4,4,1,1024]{3,2,1,0:T(1,128)S(1)} %get-tuple-element.25), channel_id=1, source_target_pairs={{0,256},{1,257},{2,258},{3,259},{4,260},{5,261},{6,262},{7,263},{8... | collective-permute-start | bytes 196616 | tf_op jit(solution)/shard_map/ppermute | solution.py:19
  113.7 9.0 %collective-permute-start.22 = (f32[1,4,10,1024]{3,2,1,0:T(8,128)S(1)}, f32[1,4,10,1024]{3,2,1,0:T(8,128)S(1)}, u32[]{:S(2)}, u32[]{:S(2)}) collective-permute-start(f32[1,4,10,1024]{3,2,1,0:T(8,128)S(1)} %get-tuple-element.18), channel_id=1, source_target_pairs={{32,0},{64,32},{96,64},{128,96},{160,128},{192,160},{224,192},{33,... | collective-permute-start | bytes 491528 | tf_op jit(solution)/shard_map/ppermute | solution.py:22
  118.9 8.3 %collective-permute-start.21 = (f32[1,4,10,1024]{3,2,1,0:T(8,128)S(1)}, f32[1,4,10,1024]{3,2,1,0:T(8,128)S(1)}, u32[]{:S(2)}, u32[]{:S(2)}) collective-permute-start(f32[1,4,10,1024]{3,2,1,0:T(8,128)S(1)} %get-tuple-element.17), channel_id=1, source_target_pairs={{0,32},{32,64},{64,96},{96,128},{128,160},{160,192},{192,224},{1,3... | collective-permute-start | bytes 491528 | tf_op jit(solution)/shard_map/ppermute | solution.py:19
  128.0 7.5 %collective-permute-start.24 = (f32[6,1,10,1024]{3,2,1,0:T(8,128)}, f32[6,1,10,1024]{3,2,1,0:T(8,128)S(1)}, u32[]{:S(2)}, u32[]{:S(2)}) collective-permute-start(f32[6,1,10,1024]{3,2,1,0:T(8,128)} %get-tuple-element.10), channel_id=1, source_target_pairs={{1,0},{2,1},{3,2},{4,3},{5,4},{6,5},{7,6},{8,7},{9,8},{10,9},{11,1... | collective-permute-start | bytes 737288 | tf_op jit(solution)/shard_map/ppermute | solution.py:22
  129.9 11.3 %collective-permute-start.23 = (f32[6,1,10,1024]{3,2,1,0:T(8,128)S(1)}, f32[6,1,10,1024]{3,2,1,0:T(8,128)S(1)}, u32[]{:S(2)}, u32[]{:S(2)}) collective-permute-start(f32[6,1,10,1024]{3,2,1,0:T(8,128)S(1)} %get-tuple-element.9), channel_id=1, source_target_pairs={{0,1},{1,2},{2,3},{3,4},{4,5},{5,6},{6,7},{7,8},{8,9},{9,10},{10,1... | collective-permute-start | bytes 737288 | tf_op jit(solution)/shard_map/ppermute | solution.py:19
  157.9 7.8 %collective-permute-start.25 = (f32[4,4,1152]{2,1,0:T(4,128)S(1)}, f32[4,4,1152]{2,1,0:T(4,128)S(1)}, u32[]{:S(2)}, u32[]{:S(2)}) collective-permute-start(f32[4,4,1152]{2,1,0:T(4,128)S(1)} %concatenate.55), channel_id=1, source_target_pairs={{0,256},{256,0},{1,257},{257,1},{2,258},{258,2},{3,259},{259,3},{4... | collective-permute-start | bytes 221192 | tf_op jit(solution)/shard_map/ppermute | solution.py:152

commit v2 on v1

--- a/solution.py
+++ b/solution.py
@@ -5,59 +5,232 @@
 from jax.experimental.pallas import tpu as pltpu
 from jax.sharding import PartitionSpec as P
 
+T = 1024
 ITERS = 3
-
-
 damping = 0.05
-
-
-def extended(block, sides, width):
-    for axis, dim in sides:
-        count = lax.axis_size(axis)
-        forward = [(i, i + 1) for i in range(count - 1)]
-        backward = [(target, source) for source, target in forward]
-        low = lax.ppermute(
-            lax.slice_in_dim(block, block.shape[dim] - width, None, axis=dim), axis, forward
-        )
-        high = lax.ppermute(lax.slice_in_dim(block, 0, width, axis=dim), axis, backward)
-        block = jnp.concatenate([low, block, high], axis=dim)
-    return block
-
-
-def passed_along(x, axis, by):
-    devices = lax.axis_size(axis)
-    pairs = [(i, i + by) for i in range(devices) if 0 <= i + by < devices]
-    return lax.ppermute(x, axis, pairs)
-
-
-def weighted_box(padded, axis):
-    length = padded.shape[axis] - 2
-    left = lax.slice_in_dim(padded, 0, length, axis=axis)
-    middle = lax.slice_in_dim(padded, 1, length + 1, axis=axis)
-    right = lax.slice_in_dim(padded, 2, length + 2, axis=axis)
-    return 0.25 * left + 0.5 * middle + 0.25 * right
-
-
-def padded_along(field, axis):
-    widths = [(0, 0)] * field.ndim
-    widths[axis] = (1, 1)
-    return jnp.pad(field, widths)
-
-
-def smooth(field):
-    field = weighted_box(padded_along(field, 3), 3)
-    padded = extended(field, (("off", 2), ("il", 0), ("xl", 1)), 1)
-    padded = weighted_box(padded, 0)
-    padded = weighted_box(padded, 1)
-    return weighted_box(padded, 2)
-
-
-def time_derivative(field):
-    padded = padded_along(field, 3)
-    return 0.5 * (padded[..., 2:] - padded[..., :-2])
-
-
-T = 1024
+MESH = pl.DeviceIdType.MESH
+STEPS = [(di, dj) for di in (-1, 0, 1) for dj in (-1, 0, 1)]
+SOURCE = {-1: slice(0, 1), 0: slice(0, 4), 1: slice(3, 4)}
+INNER = {-1: slice(1, 2), 0: slice(1, 5), 1: slice(4, 5)}
+TARGET = {-1: slice(5, 6), 0: slice(1, 5), 1: slice(0, 1)}
+
+
+def earlier(x, axis):
+    n = x.shape[axis]
+    at = lax.broadcasted_iota(jnp.int32, x.shape, axis)
+    return jnp.where(at == 0, 0.0, pltpu.roll(x, 1, axis))
+
+
+def later(x, axis):
+    n = x.shape[axis]
+    at = lax.broadcasted_iota(jnp.int32, x.shape, axis)
+    return jnp.where(at == n - 1, 0.0, pltpu.roll(x, n - 1, axis))
+
+
+def slope_kernel(counts, data_ref, out_ref, dx, d0, d1, p0, p1, gg, gr, hgg, hgr, grad, res,
+                 rden, ub, uc, q2x, q2o, q3x, q3o, pq, load_sem, send_sems, recv_sems):
+    n_il, n_xl = counts
+    off, il, xl = lax.axis_index("off"), lax.axis_index("il"), lax.axis_index("xl")
+    first = off == 0
+
+    def exists(di, dj):
+        i, j = il + di, xl + dj
+        return (i >= 0) & (i < n_il) & (j >= 0) & (j < n_xl)
+
+    def transfers(turn, field, planes):
+        made = []
+        for k, (di, dj) in enumerate(STEPS):
+            kinds = []
+            if (di, dj) != (0, 0):
+                kinds.append((k, off, None, field.at[INNER[di], INNER[dj]],
+                              field.at[TARGET[di], TARGET[dj]]))
+            for n, (source, target, sender) in enumerate(planes):
+                kinds.append((9 + 9 * n + k, 1 - off, sender, source.at[SOURCE[di], SOURCE[dj]],
+                              target.at[TARGET[di], TARGET[dj]]))
+            for slot, to_off, sender, source, target in kinds:
+                copy = pltpu.make_async_remote_copy(
+                    src_ref=source, dst_ref=target,
+                    send_sem=send_sems.at[turn, slot], recv_sem=recv_sems.at[turn, slot],
+                    device_id={"off": to_off, "il": il + di, "xl": xl + dj},
+                    device_id_type=MESH)
+                sends, takes = exists(di, dj), exists(-di, -dj)
+                if sender is not None:
+                    sends, takes = sends & (off == sender), takes & (off == 1 - sender)
+                made.append((sends, takes, copy))
+        return made
+
+    def when_all(made, which, act):
+        for item in made:
+            @pl.when(item[which])
+            def _():
+                getattr(item[2], act)()
+
+    load = pltpu.make_async_copy(data_ref, dx.at[1:5, 1:5], load_sem)
+    load.start()
+    barrier = pltpu.get_barrier_semaphore()
+    for di, dj in STEPS:
+        for o in (0, 1):
+            if (di, dj, o) != (0, 0, 0):
+                @pl.when(exists(di, dj))
+                def _():
+                    pl.semaphore_signal(
+                        barrier, inc=1, device_id_type=MESH,
+                        device_id={"off": (off + o) % 2, "il": il + di, "xl": xl + dj})
+    rows_near = 1 + (il > 0).astype(jnp.int32) + (il < n_il - 1).astype(jnp.int32)
+    cols_near = 1 + (xl > 0).astype(jnp.int32) + (xl < n_xl - 1).astype(jnp.int32)
+
+    full = [(dx, (d0, d1)), (q2x, (q2o,)), (q3x, (q3o,))]
+    for field, planes in full:
+        for di, dj in STEPS:
+            if (di, dj) != (0, 0):
+                @pl.when(jnp.logical_not(exists(-di, -dj)))
+                def _():
+                    shape = field.at[TARGET[di], TARGET[dj]].shape
+                    field[TARGET[di], TARGET[dj]] = jnp.zeros(shape, jnp.float32)
+                    for plane in planes:
+                        shape = plane.at[TARGET[di], TARGET[dj]].shape
+                        plane[TARGET[di], TARGET[dj]] = jnp.zeros(shape, jnp.float32)
+
+    load.wait()
+    for i in range(4):
+        for j in range(4):
+            tile = dx[1 + i, 1 + j]
+            p0[i, j:j + 1] = jnp.where(first, tile[7:8], tile[0:1])
+            p1[i, j:j + 1] = tile[1:2]
+    pl.semaphore_wait(barrier, 2 * rows_near * cols_near - 1)
+
+    round1 = transfers(0, dx, [(p0, d0, None), (p1, d1, 1)])
+    when_all(round1, 0, "start")
+    when_all(round1, 1, "wait_recv")
+
+    @pl.when(off == 1)
+    def _():
+        for i in range(6):
+            for j in range(6):
+                d1[i, j:j + 1] = dx[i, j, 0:1]
+
+    keep_next = jnp.where(first, 1.0, 0.0)
+    keep_before = 1.0 - keep_next
+    row8 = lax.broadcasted_iota(jnp.int32, (8, T), 0)
+
+    def gradients(i, carry):
+        for j in range(6):
+            d = dx[i, j]
+            edge = jnp.broadcast_to(d0[i, j:j + 1] * keep_next, (8, T))
+            f = jnp.where(row8 == 7, edge, pltpu.roll(d, 7, 0))
+            r = f - d
+            s = d + f
+            g = 0.25 * (later(s, 1) - earlier(s, 1))
+            gg[i, j] = g * g
+            gr[i, j] = g * r
+            grad[i, j] = g
+            res[i, j] = r
+        d, f = d0[i], d1[i]
+        s = d + f
+        g = 0.25 * (later(s, 1) - earlier(s, 1))
+        hgg[i] = g * g
+        hgr[i] = g * (f - d)
+        return carry
+
+    lax.fori_loop(0, 6, gradients, 0)
+
+    row = lax.broadcasted_iota(jnp.int32, (8, 128), 0)
+
+    def smooth_space(field, plane, out):
+        def column(c, carry):
+            lanes = pl.ds(pl.multiple_of(c * 128, 128), 128)
+            sums = []
+            for i in range(6):
+                tiles = [field[i, j, :, lanes] for j in range(6)]
+                pairs = [tiles[j] + tiles[j + 1] for j in range(5)]
+                sums.append([pairs[j] + pairs[j + 1] for j in range(4)])
+            halo = [plane[i, :, lanes] for i in range(6)]
+            for i in range(4):
+                h = halo[i] + 2.0 * halo[i + 1] + halo[i + 2]
+                h = pltpu.roll(h, 1, 0) + 2.0 * h + pltpu.roll(h, 7, 0)
+                before = h * keep_before
+                after = h * keep_next
+                for j in range(4):
+                    x = sums[i][j] + 2.0 * sums[i + 1][j] + sums[i + 2][j]
+                    up = jnp.broadcast_to(before[j + 1:j + 2], (8, 128))
+                    down = jnp.broadcast_to(after[j + 1:j + 2], (8, 128))
+                    up = jnp.where(row == 0, up, pltpu.roll(x, 1, 0))
+                    down = jnp.where(row == 7, down, pltpu.roll(x, 7, 0))
+                    out[i, j, :, lanes] = up + 2.0 * x + down
+            return carry
+        lax.fori_loop(0, 8, column, 0)
+
+    def smooth_time(u):
+        return (earlier(u, 1) + 2.0 * u + later(u, 1)) * (1.0 / 256.0)
+
+    smooth_space(gg, hgg, ub)
+    smooth_space(gr, hgr, uc)
+
+    def start_slope(i, carry):
+        for j in range(4):
+            inverse = 1.0 / (smooth_time(ub[i, j]) + damping)
+            rden[i, j] = inverse
+            slope = -smooth_time(uc[i, j]) * inverse
+            out_ref[i, j] = slope
+            g = grad[i + 1, j + 1]
+            q = g * (res[i + 1, j + 1] + slope * g)
+            q2x[i + 1, j + 1] = q
+            pq[0, i, j:j + 1] = jnp.where(first, q[7:8], q[0:1])
+        return carry
+
+    lax.fori_loop(0, 4, start_slope, 0)
+    round2 = transfers(1, q2x, [(pq.at[0], q2o, None)])
+    when_all(round2, 0, "start")
+    when_all(round2, 1, "wait_recv")
+    smooth_space(q2x, q2o, ub)
+
+    def next_slope(i, carry):
+        for j in range(4):
+            slope = out_ref[i, j] - smooth_time(ub[i, j]) * rden[i, j]
+            out_ref[i, j] = slope
+            g = grad[i + 1, j + 1]
+            q = g * (res[i + 1, j + 1] + slope * g)
+            q3x[i + 1, j + 1] = q
+            pq[1, i, j:j + 1] = jnp.where(first, q[7:8], q[0:1])
+        return carry
+
+    lax.fori_loop(0, 4, next_slope, 0)
+    round3 = transfers(2, q3x, [(pq.at[1], q3o, None)])
+    when_all(round3, 0, "start")
+    when_all(round3, 1, "wait_recv")
+    smooth_space(q3x, q3o, ub)
+
+    def last_slope(i, carry):
+        for j in range(4):
+            out_ref[i, j] = out_ref[i, j] - smooth_time(ub[i, j]) * rden[i, j]
+        return carry
+
+    lax.fori_loop(0, 4, last_slope, 0)
+    for made in (round1, round2, round3):
+        when_all(made, 0, "wait_send")
+
+
+def estimate(data, counts):
+    tiles = pltpu.VMEM((6, 6, 8, T), jnp.float32)
+    plane = pltpu.VMEM((6, 8, T), jnp.float32)
+    own = pltpu.VMEM((4, 4, 8, T), jnp.float32)
+    rows = pltpu.VMEM((4, 8, T), jnp.float32)
+    return pl.pallas_call(
+        lambda *refs: slope_kernel(counts, *refs),
+        out_shape=jax.ShapeDtypeStruct((4, 4, 8, T), jnp.float32),
+        in_specs=[pl.BlockSpec(memory_space=pl.ANY)],
+        out_specs=pl.BlockSpec(memory_space=pltpu.VMEM),
+        scratch_shapes=[tiles, plane, plane, rows, rows, tiles, tiles, plane, plane, tiles, tiles,
+                        own, own, own, tiles, plane, tiles, plane,
+                        pltpu.VMEM((2, 4, 8, T), jnp.float32),
+                        pltpu.SemaphoreType.DMA, pltpu.SemaphoreType.DMA((3, 27)),
+                        pltpu.SemaphoreType.DMA((3, 27))],
+        compiler_params=pltpu.CompilerParams(
+            collective_id=0, has_side_effects=True, vmem_limit_bytes=48 * 2**20),
+        name="slope",
+    )(data)
+
+
 NA = 16
 NB = 64
 KC = 512
@@ -132,18 +305,9 @@
     )(first, w, data, slope)
 
 
-def shards(data, offset_weight):
-    local_offsets = data.shape[2]
-    samples = data.shape[3]
-    next_rows = passed_along(data[:, :, :1, :], "off", -1)
-    following = jnp.concatenate([data[:, :, 1:, :], next_rows], axis=2)
-    residual = following - data
-    gradient = 0.5 * (time_derivative(data) + time_derivative(following))
-    denominator = smooth(gradient * gradient) + damping
-    slope = jnp.zeros_like(data)
-    for step in range(ITERS):
-        slope = slope - smooth(gradient * (residual + slope * gradient)) / denominator
-    first_offset = (lax.axis_index("off") * local_offsets).astype(jnp.float32)
+def shards(data, offset_weight, counts):
+    slope = estimate(data, counts)
+    first_offset = (lax.axis_index("off") * 8).astype(jnp.float32)
     partial = moveout(
         first_offset.reshape(1), offset_weight.reshape(8, 1),
         data.reshape(16, 8, T), slope.reshape(16, 8, T))
@@ -155,8 +319,9 @@
 
 
 def solution(mesh):
+    counts = (mesh.shape["il"], mesh.shape["xl"])
     return jax.shard_map(
-        shards,
+        lambda data, offset_weight: shards(data, offset_weight, counts),
         mesh=mesh,
         in_specs=(P("il", "xl", "off", None), P("off")),
         out_specs=(P("il", "xl", "off", None), P("il", "xl", None)),

time: 168 us -> 73.8 us (0.44)
  the two profiles are of different devices: /device:TPU:46 before, /device:TPU:22 now
where the time goes in v2:
time: 73.8 us; the launch traced here: 73.5 us
  Pallas kernels  57.6 us (78%)
  local copies, waits for them, and re-layouts  5.53 us (7%)
  waiting for transfers between devices  4.46 us (6%)
  starting transfers between devices  3.28 us (4%)
  other arithmetic  1.89 us (3%)
    pallas_call x1, Pallas kernels, estimate(): pl.pallas_call(lambda *refs: slope_kernel(counts, *refs), out_shape=jax.S...  44.3 us
    pallas_call x1, Pallas kernels, moveout(): pl.pallas_call(moveout_kernel, out_shape=jax.ShapeDtypeStruct((16, 8, 128...  13.4 us
    ppermute x1, waiting for transfers between devices, shards(): total = packed + lax.ppermute(packed, 'off', [(0, 1), (1, 0)])  4.46 us
    ppermute x1, starting transfers between devices, shards(): total = packed + lax.ppermute(packed, 'off', [(0, 1), (1, 0)])  3.28 us
    unnamed x9, local copies, waits for them, and re-layouts  3.27 us
  transfers between devices with their start and end apart: 1, of which 1 were waited for; matrix products, arithmetic and copies ran while one was open for 0% of the time, Pallas kernels for 0%

profile of v2, /device:TPU:22, one launch (start us, length us, event | category | flops | bytes accessed | tf_op | source)
XLA Modules:
  0.0 73.5 jit_solution(2397416235033135194)
XLA Ops:
  0.6 0.0 copy-start.3
  0.6 0.6 copy-done.3
  1.3 0.6 reduce_sum.9
  1.9 0.7 copy.5.w_ref
  2.6 0.0 copy-start.2
  2.6 1.0 %copy-done.2 = f32[4,4,8,1024]{3,2,1,0:T(8,128)S(1)} copy-done((f32[4,4,8,1024]{3,2,1,0:T(8,128)S(1)}, f32[4,4,8,1024]{3,2,1,0:T(8,128)}, u32[]{:S(2)}) %copy-start.2) | copy-done | bytes 524312
  3.6 44.3 %slope.1 = f32[4,4,8,1024]{3,2,1,0:T(8,128)S(1)} custom-call(f32[4,4,8,1024]{3,2,1,0:T(8,128)S(1)} %copy-done.2), custom_call_target="tpu_custom_call" | custom-call | tf_op jit(solution)/shard_map/slope/pallas_call | solution.py:218
  47.9 0.0 copy-start
  47.9 0.8 %copy-done = f32[4,4,8,1024]{3,2,1,0:T(8,128)} copy-done((f32[4,4,8,1024]{3,2,1,0:T(8,128)}, f32[4,4,8,1024]{3,2,1,0:T(8,128)S(1)}, u32[]{:S(2)}) %copy-start) | copy-done | bytes 524312
  48.7 13.4 %moveout.1 = f32[16,8,128]{2,1,0:T(8,128)} custom-call(f32[1]{0:T(128)} %bitcast.first_ref, f32[8,1]{1,0:T(8,128)} %copy.5.w_ref, f32[16,8,1024]{2,1,0:T(8,128)} %bitcast.5, f32[16,8,1024]{2,1,0:T(8,128)} %bitcast.4), custom_call_target="tpu_custom_call" | custom-call | tf_op jit(solution)/shard_map/moveout/pallas_call | solution.py:298
  62.0 0.0 copy-start.1
  62.0 0.9 %reshape.23 = f32[4,4,1024]{2,1,0:T(4,128)S(1)} reshape(f32[16,8,128]{2,1,0:T(8,128)} %moveout.1) | data formatting | bytes 131072 | tf_op jit(solution)/shard_map/reshape | solution.py:315
  63.0 0.6 concatenate.3
  63.6 3.3 %collective-permute-start = (f32[4,4,1152]{2,1,0:T(4,128)S(1)}, f32[4,4,1152]{2,1,0:T(4,128)S(1)}, u32[]{:S(2)}, u32[]{:S(2)}) collective-permute-start(f32[4,4,1152]{2,1,0:T(4,128)S(1)} %concatenate.3), channel_id=1, source_target_pairs={{0,256},{256,0},{1,257},{257,1},{2,258},{258,2},{3,259},{259,3},{4... | collective-permute-start | bytes 221192 | tf_op jit(solution)/shard_map/ppermute | solution.py:316
  66.8 4.5 %collective-permute-done = f32[4,4,1152]{2,1,0:T(4,128)S(1)} collective-permute-done((f32[4,4,1152]{2,1,0:T(4,128)S(1)}, f32[4,4,1152]{2,1,0:T(4,128)S(1)}, u32[]{:S(2)}, u32[]{:S(2)}) %collective-permute-start) | collective-permute-done | bytes 73760 | tf_op jit(solution)/shard_map/ppermute | solution.py:316
  71.3 0.6 pad_add_fusion
  71.9 0.1 slice_reduce_fusion
  72.0 0.7 slice_divide_fusion
  72.7 0.0 copy-done.1
  72.7 0.8 %copy.7 = f32[4,4,8,1024]{3,2,1,0:T(8,128)} copy(f32[4,4,8,1024]{3,2,1,0:T(8,128)S(1)} %copy-done.1) | data formatting | bytes 1048576
Async XLA Ops:
  0.6 0.7 copy-start.3
  2.6 1.0 %copy-start.2 = (f32[4,4,8,1024]{3,2,1,0:T(8,128)S(1)}, f32[4,4,8,1024]{3,2,1,0:T(8,128)}, u32[]{:S(2)}) copy-start(f32[4,4,8,1024]{3,2,1,0:T(8,128)} %refs_0_.1) | copy-start | bytes 1572868
  47.9 0.8 %copy-start = (f32[4,4,8,1024]{3,2,1,0:T(8,128)}, f32[4,4,8,1024]{3,2,1,0:T(8,128)S(1)}, u32[]{:S(2)}) copy-start(f32[4,4,8,1024]{3,2,1,0:T(8,128)S(1)} %slope.1) | copy-start | bytes 1572868
  62.0 10.7 %copy-start.1 = (f32[4,4,8,1024]{3,2,1,0:T(8,128)S(1)}, f32[4,4,8,1024]{3,2,1,0:T(8,128)}, u32[]{:S(2)}) copy-start(f32[4,4,8,1024]{3,2,1,0:T(8,128)} %copy-done) | copy-start | bytes 1572868
  63.6 7.8 %collective-permute-start = (f32[4,4,1152]{2,1,0:T(4,128)S(1)}, f32[4,4,1152]{2,1,0:T(4,128)S(1)}, u32[]{:S(2)}, u32[]{:S(2)}) collective-permute-start(f32[4,4,1152]{2,1,0:T(4,128)S(1)} %concatenate.3), channel_id=1, source_target_pairs={{0,256},{256,0},{1,257},{257,1},{2,258},{258,2},{3,259},{259,3},{4... | collective-permute-start | bytes 221192 | tf_op jit(solution)/shard_map/ppermute | solution.py:316

commit v3 on v2

--- a/solution.py
+++ b/solution.py
@@ -6,7 +6,8 @@
 from jax.sharding import PartitionSpec as P
 
 T = 1024
-ITERS = 3
+NA = 16
+NB = 64
 damping = 0.05
 MESH = pl.DeviceIdType.MESH
 STEPS = [(di, dj) for di in (-1, 0, 1) for dj in (-1, 0, 1)]
@@ -27,8 +28,10 @@
     return jnp.where(at == n - 1, 0.0, pltpu.roll(x, n - 1, axis))
 
 
-def slope_kernel(counts, data_ref, out_ref, dx, d0, d1, p0, p1, gg, gr, hgg, hgr, grad, res,
-                 rden, ub, uc, q2x, q2o, q3x, q3o, pq, load_sem, send_sems, recv_sems):
+def moveout_kernel(counts, weight_hbm, data_ref, out_ref, stack_ref, dx, d0, d1, p0, p1, gg, gr,
+                   hgg, hgr, grad, res, rden, ub, uc, q2x, q2o, q3x, q3o, pq, wsum, raw, part,
+                   load_sem, send_sems, recv_sems, sum_sems, part_sems, weight_ref,
+                   weight_sem, slopes, slope_sems):
     n_il, n_xl = counts
     off, il, xl = lax.axis_index("off"), lax.axis_index("il"), lax.axis_index("xl")
     first = off == 0
@@ -67,6 +70,8 @@
 
     load = pltpu.make_async_copy(data_ref, dx.at[1:5, 1:5], load_sem)
     load.start()
+    load_weight = pltpu.make_async_copy(weight_hbm, weight_ref, weight_sem)
+    load_weight.start()
     barrier = pltpu.get_barrier_semaphore()
     for di, dj in STEPS:
         for o in (0, 1):
@@ -91,6 +96,11 @@
                         shape = plane.at[TARGET[di], TARGET[dj]].shape
                         plane[TARGET[di], TARGET[dj]] = jnp.zeros(shape, jnp.float32)
 
+    load_weight.wait()
+    total = weight_ref[0]
+    for h in range(1, 8):
+        total = total + weight_ref[h]
+    wsum[0] = jnp.full((8, 128), total, jnp.float32)
     load.wait()
     for i in range(4):
         for j in range(4):
@@ -99,8 +109,13 @@
             p1[i, j:j + 1] = tile[1:2]
     pl.semaphore_wait(barrier, 2 * rows_near * cols_near - 1)
 
+    partner = {"off": 1 - off, "il": il, "xl": xl}
     round1 = transfers(0, dx, [(p0, d0, None), (p1, d1, 1)])
     when_all(round1, 0, "start")
+    sums = pltpu.make_async_remote_copy(
+        src_ref=wsum.at[0], dst_ref=wsum.at[1], send_sem=sum_sems.at[0], recv_sem=sum_sems.at[1],
+        device_id=partner, device_id_type=MESH)
+    sums.start()
     when_all(round1, 1, "wait_recv")
 
     @pl.when(off == 1)
@@ -171,7 +186,7 @@
             inverse = 1.0 / (smooth_time(ub[i, j]) + damping)
             rden[i, j] = inverse
             slope = -smooth_time(uc[i, j]) * inverse
-            out_ref[i, j] = slope
+            slopes[i, j] = slope
             g = grad[i + 1, j + 1]
             q = g * (res[i + 1, j + 1] + slope * g)
             q2x[i + 1, j + 1] = q
@@ -186,8 +201,8 @@
 
     def next_slope(i, carry):
         for j in range(4):
-            slope = out_ref[i, j] - smooth_time(ub[i, j]) * rden[i, j]
-            out_ref[i, j] = slope
+            slope = slopes[i, j] - smooth_time(ub[i, j]) * rden[i, j]
+            slopes[i, j] = slope
             g = grad[i + 1, j + 1]
             q = g * (res[i + 1, j + 1] + slope * g)
             q3x[i + 1, j + 1] = q
@@ -200,67 +215,34 @@
     when_all(round3, 1, "wait_recv")
     smooth_space(q3x, q3o, ub)
 
-    def last_slope(i, carry):
-        for j in range(4):
-            out_ref[i, j] = out_ref[i, j] - smooth_time(ub[i, j]) * rden[i, j]
-        return carry
-
-    lax.fori_loop(0, 4, last_slope, 0)
-    for made in (round1, round2, round3):
-        when_all(made, 0, "wait_send")
-
-
-def estimate(data, counts):
-    tiles = pltpu.VMEM((6, 6, 8, T), jnp.float32)
-    plane = pltpu.VMEM((6, 8, T), jnp.float32)
-    own = pltpu.VMEM((4, 4, 8, T), jnp.float32)
-    rows = pltpu.VMEM((4, 8, T), jnp.float32)
-    return pl.pallas_call(
-        lambda *refs: slope_kernel(counts, *refs),
-        out_shape=jax.ShapeDtypeStruct((4, 4, 8, T), jnp.float32),
-        in_specs=[pl.BlockSpec(memory_space=pl.ANY)],
-        out_specs=pl.BlockSpec(memory_space=pltpu.VMEM),
-        scratch_shapes=[tiles, plane, plane, rows, rows, tiles, tiles, plane, plane, tiles, tiles,
-                        own, own, own, tiles, plane, tiles, plane,
-                        pltpu.VMEM((2, 4, 8, T), jnp.float32),
-                        pltpu.SemaphoreType.DMA, pltpu.SemaphoreType.DMA((3, 27)),
-                        pltpu.SemaphoreType.DMA((3, 27))],
-        compiler_params=pltpu.CompilerParams(
-            collective_id=0, has_side_effects=True, vmem_limit_bytes=48 * 2**20),
-        name="slope",
-    )(data)
-
-
-NA = 16
-NB = 64
-KC = 512
-
-
-def moveout_kernel(first_ref, w_ref, data_ref, slope_ref, out_ref):
     tt = lax.broadcasted_iota(jnp.int32, (8, T), 1).astype(jnp.float32) + 1.0
-    hh = lax.broadcasted_iota(jnp.int32, (8, T), 0).astype(jnp.float32) + (0.5 + first_ref[0])
+    hh = lax.broadcasted_iota(jnp.int32, (8, T), 0).astype(jnp.float32) + 0.5
+    hh = hh + jnp.where(first, 0.0, 8.0)
     tth = tt * hh
     ttq = tt * tt
-    w = w_ref[...]
-    rows = lax.broadcasted_iota(jnp.int32, (NA, 128), 0)
-    rows = jnp.where(rows < 8, 2 * rows, 2 * rows - 15)
-    ia = rows.astype(jnp.float32).astype(jnp.bfloat16)
-    ib = lax.broadcasted_iota(jnp.int32, (NB, 128), 0).astype(jnp.float32).astype(jnp.bfloat16)
-    zero = jnp.zeros((NA, 128), jnp.bfloat16)
+    weight = jnp.full((8, 128), weight_ref[0], jnp.float32)
+    for h in range(1, 8):
+        weight = jnp.where(row == h, weight_ref[h], weight)
+    weight = jnp.concatenate([weight] * 8, axis=1)
+    high = lax.broadcasted_iota(jnp.int32, (NA, 128), 0)
+    high = jnp.where(high < 8, 2 * high, 2 * high - 15)
+    high = high.astype(jnp.float32).astype(jnp.bfloat16)
+    low = lax.broadcasted_iota(jnp.int32, (NB, 128), 0).astype(jnp.float32).astype(jnp.bfloat16)
+    zero_a = jnp.zeros((NA, 128), jnp.bfloat16)
+    zero_b = jnp.zeros((NB, 128), jnp.bfloat16)
     one_b = jnp.ones((NB, 128), jnp.bfloat16)
-    zero_b = jnp.zeros((NB, 128), jnp.bfloat16)
     lane = lax.broadcasted_iota(jnp.int32, (8, 128), 1)
-    row = lax.broadcasted_iota(jnp.int32, (8, 128), 0)
-
-    def midpoint(m, carry):
-        s = slope_ref[m]
-        place = jnp.sqrt(jnp.maximum(ttq - tth * s, 1.0)) - 1.0
-        low = jnp.floor(place)
-        f = place - low
-        idx = jnp.minimum(low, float(T))
-        a = jnp.floor(idx * (1.0 / NB))
-        b = idx - a * NB
-        v = data_ref[m] * w
+
+    def push(i, j, at):
+        slope = slopes[i, j] - smooth_time(ub[i, j]) * rden[i, j]
+        slopes[i, j] = slope
+        place = jnp.sqrt(jnp.maximum(ttq - tth * slope, 1.0)) - 1.0
+        cell = jnp.floor(place)
+        f = place - cell
+        cell = jnp.minimum(cell, float(T))
+        a = jnp.floor(cell * (1.0 / NB))
+        b = cell - a * NB
+        v = dx[1 + i, 1 + j] * weight
         x1 = v * f
         x0 = v - x1
         x0h = x0.astype(jnp.bfloat16).astype(jnp.float32)
@@ -268,19 +250,23 @@
         values = (x0h, x0 - x0h, x1h, x1 - x1h)
         acc = jnp.zeros((4 * NA, NB), jnp.float32)
         for h in range(8):
-            for c in range(0, T, KC):
-                left, right = [], []
-                for l in range(c, c + KC, 128):
-                    def spread(x, n):
-                        part = x[h:h + 1, l:l + 128]
-                        return jnp.broadcast_to(part, (n, 128)).astype(jnp.bfloat16)
-                    hit = spread(a, NA) == ia
-                    left.append(jnp.concatenate(
-                        [jnp.where(hit, spread(x, NA), zero) for x in values], axis=0))
-                    right.append(jnp.where(spread(b, NB) == ib, one_b, zero_b))
-                acc = acc + lax.dot_general(
-                    jnp.concatenate(left, axis=1), jnp.concatenate(right, axis=1),
-                    (((1,), (1,)), ((), ())), preferred_element_type=jnp.float32)
+            left, right = [], []
+            for c in range(0, T, 128):
+                def spread(x, n):
+                    part_of = x[h:h + 1, c:c + 128]
+                    return jnp.broadcast_to(part_of, (n, 128)).astype(jnp.bfloat16)
+                hit = spread(a, NA) == high
+                left.append(jnp.concatenate(
+                    [jnp.where(hit, spread(x, NA), zero_a) for x in values], axis=0))
+                right.append(jnp.where(spread(b, NB) == low, one_b, zero_b))
+            dot = lax.dot_general(
+                jnp.concatenate(left, axis=1), jnp.concatenate(right, axis=1),
+                (((1,), (1,)), ((), ())), preferred_element_type=jnp.float32)
+            acc = acc + jnp.maximum(dot, -3.0e38)
+        raw[at] = acc
+
+    def gather(at):
+        acc = raw[at]
         lower = acc[:NA] + acc[NA:2 * NA]
         upper = acc[2 * NA:3 * NA] + acc[3 * NA:]
         lower = jnp.concatenate([lower[:8], lower[8:]], axis=1)
@@ -288,40 +274,78 @@
         upper = pltpu.roll(upper, 1, 1)
         before = pltpu.roll(upper, 1, 0)
         upper = jnp.where(lane == 0, jnp.where(row == 0, 0.0, before), upper)
-        out_ref[m] = lower + upper
+        part[0, at] = lower + upper
+
+    def exchange(n):
+        return pltpu.make_async_remote_copy(
+            src_ref=part.at[0, 4 * n:4 * n + 4], dst_ref=part.at[1, 4 * n:4 * n + 4],
+            send_sem=part_sems.at[0, n], recv_sem=part_sems.at[1, n],
+            device_id=partner, device_id_type=MESH)
+
+    def store(i):
+        return pltpu.make_async_copy(slopes.at[i], out_ref.at[i], slope_sems.at[i])
+
+    def push_row(i, carry):
+        for j in range(4):
+            push(i, j, 4 * i + j)
+        store(i).start()
         return carry
 
-    lax.fori_loop(0, 16, midpoint, 0)
-
-
-def moveout(first, w, data, slope):
+    lax.fori_loop(0, 4, push_row, 0)
+    for n in range(4):
+        for at in range(4 * n, 4 * n + 4):
+            gather(at)
+        exchange(n).start()
+    sums.wait_recv()
+    weights = wsum[0] + wsum[1]
+    for n in range(4):
+        exchange(n).wait_recv()
+        for at in range(4 * n, 4 * n + 4):
+            stack_ref[at] = (part[0, at] + part[1, at]) / weights
+    sums.wait_send()
+    for n in range(4):
+        exchange(n).wait_send()
+        store(n).wait()
+    for made in (round1, round2, round3):
+        when_all(made, 0, "wait_send")
+
+
+def moveout(data, offset_weight, counts):
+    tiles = pltpu.VMEM((6, 6, 8, T), jnp.float32)
+    plane = pltpu.VMEM((6, 8, T), jnp.float32)
+    own = pltpu.VMEM((4, 4, 8, T), jnp.float32)
+    rows = pltpu.VMEM((4, 8, T), jnp.float32)
     return pl.pallas_call(
-        moveout_kernel,
-        out_shape=jax.ShapeDtypeStruct((16, 8, 128), jnp.float32),
-        in_specs=[pl.BlockSpec(memory_space=pltpu.SMEM)]
-        + [pl.BlockSpec(memory_space=pltpu.VMEM)] * 3,
-        out_specs=pl.BlockSpec(memory_space=pltpu.VMEM),
+        lambda *refs: moveout_kernel(counts, *refs),
+        out_shape=(jax.ShapeDtypeStruct((4, 4, 8, T), jnp.float32),
+                   jax.ShapeDtypeStruct((16, 8, 128), jnp.float32)),
+        in_specs=[pl.BlockSpec(memory_space=pltpu.HBM)] * 2,
+        out_specs=(pl.BlockSpec(memory_space=pltpu.HBM), pl.BlockSpec(memory_space=pltpu.VMEM)),
+        scratch_shapes=[tiles, plane, plane, rows, rows, tiles, tiles, plane, plane, tiles, tiles,
+                        own, own, own, tiles, plane, tiles, plane,
+                        pltpu.VMEM((2, 4, 8, T), jnp.float32),
+                        pltpu.VMEM((2, 8, 128), jnp.float32),
+                        pltpu.VMEM((16, 4 * NA, NB), jnp.float32),
+                        pltpu.VMEM((2, 16, 8, 128), jnp.float32),
+                        pltpu.SemaphoreType.DMA, pltpu.SemaphoreType.DMA((3, 27)),
+                        pltpu.SemaphoreType.DMA((3, 27)), pltpu.SemaphoreType.DMA((2,)),
+                        pltpu.SemaphoreType.DMA((2, 4)), pltpu.SMEM((8,), jnp.float32),
+                        pltpu.SemaphoreType.DMA, own, pltpu.SemaphoreType.DMA((4,))],
+        compiler_params=pltpu.CompilerParams(
+            collective_id=0, has_side_effects=True, vmem_limit_bytes=67043328),
         name="moveout",
-    )(first, w, data, slope)
-
-
-def shards(data, offset_weight, counts):
-    slope = estimate(data, counts)
-    first_offset = (lax.axis_index("off") * 8).astype(jnp.float32)
-    partial = moveout(
-        first_offset.reshape(1), offset_weight.reshape(8, 1),
-        data.reshape(16, 8, T), slope.reshape(16, 8, T))
-    packed = jnp.concatenate(
-        [partial.reshape(4, 4, T), jnp.full((4, 4, 128), jnp.sum(offset_weight))], axis=2)
-    total = packed + lax.ppermute(packed, "off", [(0, 1), (1, 0)])
-    stacked = total[:, :, :T] / total[:, :, T:T + 1]
-    return (slope, stacked)
+    )(offset_weight, data)
 
 
 def solution(mesh):
     counts = (mesh.shape["il"], mesh.shape["xl"])
+
+    def shards(data, offset_weight):
+        slope, stacked = moveout(data, offset_weight, counts)
+        return slope, stacked.reshape(4, 4, T)
+
     return jax.shard_map(
-        lambda data, offset_weight: shards(data, offset_weight, counts),
+        shards,
         mesh=mesh,
         in_specs=(P("il", "xl", "off", None), P("off")),
         out_specs=(P("il", "xl", "off", None), P("il", "xl", None)),

time: 73.8 us -> 58.7 us (0.80)
  the two profiles are of different devices: /device:TPU:22 before, /device:TPU:18 now
where the time goes in v3:
time: 58.7 us; the launch traced here: 58.5 us
  Pallas kernels  54.4 us (93%)
  local copies, waits for them, and re-layouts  3.37 us (6%)
  between operations  0.64 us (1%)
    pallas_call x1, Pallas kernels, moveout(): pl.pallas_call(lambda *refs: moveout_kernel(counts, *refs), out_shape=(ja...  54.4 us
    unnamed x1, local copies, waits for them, and re-layouts  1.88 us
    reshape x1, local copies, waits for them, and re-layouts, shards(): return (slope, stacked.reshape(4, 4, T))  1.49 us

profile of v3, /device:TPU:18, one launch (start us, length us, event | category | flops | bytes accessed | tf_op | source)
XLA Modules:
  0.0 58.5 jit_solution(9104738195506085563)
XLA Ops:
  0.6 54.4 %moveout.1 = (f32[4,4,8,1024]{3,2,1,0:T(8,128)}, f32[16,8,128]{2,1,0:T(8,128)}) custom-call(f32[8]{0:T(128)} %refs_0_.1, f32[4,4,8,1024]{3,2,1,0:T(8,128)} %refs_1_.1), custom_call_target="tpu_custom_call" | custom-call | tf_op jit(solution)/shard_map/moveout/pallas_call | solution.py:318
  55.1 1.5 %reshape.7 = f32[4,4,1024]{2,1,0:T(4,128)} reshape(f32[16,8,128]{2,1,0:T(8,128)} %get-tuple-element.5) | data formatting | bytes 131072 | tf_op jit(solution)/shard_map/reshape | solution.py:345
  56.6 1.9 %copy.5 = f32[4,4,8,1024]{3,2,1,0:T(8,128)} copy(f32[4,4,8,1024]{3,2,1,0:T(8,128)} %get-tuple-element.8) | data formatting | bytes 1048576

commit v4 on v3

v4 whole, which is shorter than its diff:
```python
import jax
import jax.numpy as jnp
from jax import lax
from jax.experimental import pallas as pl
from jax.experimental.pallas import tpu as pltpu
from jax.sharding import PartitionSpec as P

T = 1024
NA = 16
NB = 64
damping = 0.05
MESH = pl.DeviceIdType.MESH
STEPS = [(di, dj) for di in (-1, 0, 1) for dj in (-1, 0, 1)]
SOURCE = {-1: slice(0, 1), 0: slice(0, 4), 1: slice(3, 4)}
INNER = {-1: slice(1, 2), 0: slice(1, 5), 1: slice(4, 5)}
TARGET = {-1: slice(5, 6), 0: slice(1, 5), 1: slice(0, 1)}
WINDOWS = ((0, 512), (384, 640))
SEAM = 448


def earlier(x, axis):
    x = pltpu.roll(x, 1, axis)
    at = lax.broadcasted_iota(jnp.int32, (8, 128), axis)
    return jnp.concatenate([jnp.where(at == 0, 0.0, x[:, :128]), x[:, 128:]], axis=1)


def later(x, axis):
    n = x.shape[axis]
    x = pltpu.roll(x, n - 1, axis)
    at = lax.broadcasted_iota(jnp.int32, (8, 128), axis)
    return jnp.concatenate([x[:, :n - 128], jnp.where(at == 127, 0.0, x[:, n - 128:])], axis=1)


def smooth_time(u):
    return (earlier(u, 1) + 2.0 * u + later(u, 1)) * (1.0 / 256.0)


def moveout_kernel(counts, weight_hbm, data_hbm, out_ref, stack_ref, *scratch):
    halves, scratch = (scratch[:20], scratch[20:40]), scratch[40:]
    (wsum, raw, part, weight_ref, weight_sem, load_sems, send_sems, recv_sems,
     sum_sems, part_sems) = scratch
    n_il, n_xl = counts
    off, il, xl = lax.axis_index("off"), lax.axis_index("il"), lax.axis_index("xl")
    first = off == 0
    partner = {"off": 1 - off, "il": il, "xl": xl}

    def exists(di, dj):
        i, j = il + di, xl + dj
        return (i >= 0) & (i < n_il) & (j >= 0) & (j < n_xl)

    def transfers(turn, field, planes):
        made = []
        for k, (di, dj) in enumerate(STEPS):
            kinds = []
            if (di, dj) != (0, 0):
                kinds.append((k, off, None, field.at[INNER[di], INNER[dj]],
                              field.at[TARGET[di], TARGET[dj]]))
            for n, (source, target, sender) in enumerate(planes):
                kinds.append((9 + 9 * n + k, 1 - off, sender, source.at[SOURCE[di], SOURCE[dj]],
                              target.at[TARGET[di], TARGET[dj]]))
            for slot, to_off, sender, source, target in kinds:
                copy = pltpu.make_async_remote_copy(
                    src_ref=source, dst_ref=target,
                    send_sem=send_sems.at[turn, slot], recv_sem=recv_sems.at[turn, slot],
                    device_id={"off": to_off, "il": il + di, "xl": xl + dj},
                    device_id_type=MESH)
                sends, takes = exists(di, dj), exists(-di, -dj)
                if sender is not None:
                    sends, takes = sends & (off == sender), takes & (off == 1 - sender)
                made.append((sends, takes, copy))
        return made

    def when_all(made, which, act):
        for item in made:
            @pl.when(item[which])
            def _():
                getattr(item[2], act)()

    loads = []
    for n, (base, width) in enumerate(WINDOWS):
        load = pltpu.make_async_copy(
            data_hbm.at[:, :, :, base:base + width], halves[n][0].at[1:5, 1:5], load_sems.at[n])
        load.start()
        loads.append(load)
    load_weight = pltpu.make_async_copy(weight_hbm, weight_ref, weight_sem)
    load_weight.start()
    barrier = pltpu.get_barrier_semaphore()
    for di, dj in STEPS:
        for o in (0, 1):
            if (di, dj, o) != (0, 0, 0):
                @pl.when(exists(di, dj))
                def _():
                    pl.semaphore_signal(
                        barrier, inc=1, device_id_type=MESH,
                        device_id={"off": (off + o) % 2, "il": il + di, "xl": xl + dj})
    rows_near = 1 + (il > 0).astype(jnp.int32) + (il < n_il - 1).astype(jnp.int32)
    cols_near = 1 + (xl > 0).astype(jnp.int32) + (xl < n_xl - 1).astype(jnp.int32)

    for dx, d0, d1, _, _, gg, gr, hgg, hgr, grad, res, rden, ub, uc, q2, o2, q3, o3, pq, own \
            in halves:
        for field, planes in ((dx, (d0, d1)), (q2, (o2,)), (q3, (o3,))):
            for di, dj in STEPS:
                if (di, dj) != (0, 0):
                    @pl.when(jnp.logical_not(exists(-di, -dj)))
                    def _():
                        for target in (field,) + planes:
                            shape = target.at[TARGET[di], TARGET[dj]].shape
                            target[TARGET[di], TARGET[dj]] = jnp.zeros(shape, jnp.float32)

    load_weight.wait()
    total = weight_ref[0]
    for h in range(1, 8):
        total = total + weight_ref[h]
    wsum[0] = jnp.full((8, 128), total, jnp.float32)
    for load, half in zip(loads, halves):
        load.wait()
        dx, p0, p1 = half[0], half[3], half[4]
        for i in range(4):
            for j in range(4):
                tile = dx[1 + i, 1 + j]
                p0[i, j:j + 1] = jnp.where(first, tile[7:8], tile[0:1])
                p1[i, j:j + 1] = tile[1:2]
    pl.semaphore_wait(barrier, 2 * rows_near * cols_near - 1)

    rounds = []
    for n, half in enumerate(halves):
        dx, d0, d1, p0, p1 = half[:5]
        made = transfers(n, dx, [(p0, d0, None), (p1, d1, 1)])
        when_all(made, 0, "start")
        rounds.append(made)
    sums = pltpu.make_async_remote_copy(
        src_ref=wsum.at[0], dst_ref=wsum.at[1], send_sem=sum_sems.at[0], recv_sem=sum_sems.at[1],
        device_id=partner, device_id_type=MESH)
    sums.start()

    keep_next = jnp.where(first, 1.0, 0.0)
    keep_before = 1.0 - keep_next
    row = lax.broadcasted_iota(jnp.int32, (8, 128), 0)
    lane = lax.broadcasted_iota(jnp.int32, (8, 128), 1)

    def smooth_space(field, plane, out):
        def column(c, carry):
            lanes = pl.ds(pl.multiple_of(c * 128, 128), 128)
            sums_xl = []
            for i in range(6):
                tiles = [field[i, j, :, lanes] for j in range(6)]
                pairs = [tiles[j] + tiles[j + 1] for j in range(5)]
                sums_xl.append([pairs[j] + pairs[j + 1] for j in range(4)])
            halo = [plane[i, :, lanes] for i in range(6)]
            for i in range(4):
                h = halo[i] + 2.0 * halo[i + 1] + halo[i + 2]
                h = pltpu.roll(h, 1, 0) + 2.0 * h + pltpu.roll(h, 7, 0)
                before = h * keep_before
                after = h * keep_next
                for j in range(4):
                    x = sums_xl[i][j] + 2.0 * sums_xl[i + 1][j] + sums_xl[i + 2][j]
                    up = jnp.broadcast_to(before[j + 1:j + 2], (8, 128))
                    down = jnp.broadcast_to(after[j + 1:j + 2], (8, 128))
                    up = jnp.where(row == 0, up, pltpu.roll(x, 1, 0))
                    down = jnp.where(row == 7, down, pltpu.roll(x, 7, 0))
                    out[i, j, :, lanes] = up + 2.0 * x + down
            return carry
        lax.fori_loop(0, field.shape[3] // 128, column, 0)

    def first_turn(n):
        dx, d0, d1, _, _, gg, gr, hgg, hgr, grad, res, rden, ub, uc, q2, o2, q3, o3, pq, own = \
            halves[n]
        width = WINDOWS[n][1]
        row8 = lax.broadcasted_iota(jnp.int32, (8, width), 0)

        @pl.when(off == 1)
        def _():
            for i in range(6):
                for j in range(6):
                    d1[i, j:j + 1] = dx[i, j, 0:1]

        def gradients(i, carry):
            for j in range(6):
                d = dx[i, j]
                edge = jnp.broadcast_to(d0[i, j:j + 1] * keep_next, (8, width))
                f = jnp.where(row8 == 7, edge, pltpu.roll(d, 7, 0))
                r = f - d
                s = d + f
                g = 0.25 * (later(s, 1) - earlier(s, 1))
                gg[i, j] = g * g
                gr[i, j] = g * r
                grad[i, j] = g
                res[i, j] = r
            d, f = d0[i], d1[i]
            s = d + f
            g = 0.25 * (later(s, 1) - earlier(s, 1))
            hgg[i] = g * g
            hgr[i] = g * (f - d)
            return carry

        lax.fori_loop(0, 6, gradients, 0)
        smooth_space(gg, hgg, ub)
        smooth_space(gr, hgr, uc)

        def start_slope(i, carry):
            for j in range(4):
                inverse = 1.0 / (smooth_time(ub[i, j]) + damping)
                rden[i, j] = inverse
                slope = -smooth_time(uc[i, j]) * inverse
                own[i, j] = slope
                g = grad[i + 1, j + 1]
                q = g * (res[i + 1, j + 1] + slope * g)
                q2[i + 1, j + 1] = q
                pq[0, i, j:j + 1] = jnp.where(first, q[7:8], q[0:1])
            return carry

        lax.fori_loop(0, 4, start_slope, 0)
        made = transfers(2 + n, q2, [(pq.at[0], o2, None)])
        when_all(made, 0, "start")
        rounds.append(made)

    def second_turn(n):
        grad, res, rden, ub, q2, o2, q3, pq, own = (halves[n][k] for k in (
            9, 10, 11, 12, 14, 15, 16, 18, 19))
        smooth_space(q2, o2, ub)

        def next_slope(i, carry):
            for j in range(4):
                slope = own[i, j] - smooth_time(ub[i, j]) * rden[i, j]
                own[i, j] = slope
                g = grad[i + 1, j + 1]
                q = g * (res[i + 1, j + 1] + slope * g)
                q3[i + 1, j + 1] = q
                pq[1, i, j:j + 1] = jnp.where(first, q[7:8], q[0:1])
            return carry

        lax.fori_loop(0, 4, next_slope, 0)
        made = transfers(4 + n, q3, [(pq.at[1], halves[n][17], None)])
        when_all(made, 0, "start")
        rounds.append(made)

    weight = jnp.full((8, 128), weight_ref[0], jnp.float32)
    for h in range(1, 8):
        weight = jnp.where(row == h, weight_ref[h], weight)
    high = lax.broadcasted_iota(jnp.int32, (NA, 128), 0)
    high = jnp.where(high < 8, 2 * high, 2 * high - 15)
    high = high.astype(jnp.float32).astype(jnp.bfloat16)
    low = lax.broadcasted_iota(jnp.int32, (NB, 128), 0).astype(jnp.float32).astype(jnp.bfloat16)
    zero_a = jnp.zeros((NA, 128), jnp.bfloat16)
    zero_b = jnp.zeros((NB, 128), jnp.bfloat16)
    one_b = jnp.ones((NB, 128), jnp.bfloat16)

    def push(data, slope, start):
        width = data.shape[1]
        tt = lax.broadcasted_iota(jnp.int32, (8, width), 1).astype(jnp.float32) + (start + 1.0)
        hh = lax.broadcasted_iota(jnp.int32, (8, width), 0).astype(jnp.float32) + 0.5
        hh = hh + 8.0 * keep_before
        place = jnp.sqrt(jnp.maximum(tt * tt - tt * hh * slope, 1.0)) - 1.0
        cell = jnp.floor(place)
        f = place - cell
        cell = jnp.minimum(cell, float(T))
        a = jnp.floor(cell * (1.0 / NB))
        b = cell - a * NB
        v = data * jnp.concatenate([weight] * (width // 128), axis=1)
        x1 = v * f
        x0 = v - x1
        x0h = x0.astype(jnp.bfloat16).astype(jnp.float32)
        x1h = x1.astype(jnp.bfloat16).astype(jnp.float32)
        values = (x0h, x0 - x0h, x1h, x1 - x1h)
        acc = jnp.zeros((4 * NA, NB), jnp.float32)
        for h in range(0, 8, 2):
            left, right = [], []
            for k in (h, h + 1):
                for c in range(0, width, 128):
                    def spread(x, n):
                        piece = x[k:k + 1, c:c + 128]
                        return jnp.broadcast_to(piece, (n, 128)).astype(jnp.bfloat16)
                    hit = spread(a, NA) == high
                    left.append(jnp.concatenate(
                        [jnp.where(hit, spread(x, NA), zero_a) for x in values], axis=0))
                    right.append(jnp.where(spread(b, NB) == low, one_b, zero_b))
            dot = lax.dot_general(
                jnp.concatenate(left, axis=1), jnp.concatenate(right, axis=1),
                (((1,), (1,)), ((), ())), preferred_element_type=jnp.float32)
            acc = acc + jnp.maximum(dot, -3.0e38)
        return acc

    def gather(i):
        for j in range(4):
            acc = raw[4 * i + j]
            lower = acc[:NA] + acc[NA:2 * NA]
            upper = acc[2 * NA:3 * NA] + acc[3 * NA:]
            lower = jnp.concatenate([lower[:8], lower[8:]], axis=1)
            upper = jnp.concatenate([upper[:8], upper[8:]], axis=1)
            upper = pltpu.roll(upper, 1, 1)
            before = pltpu.roll(upper, 1, 0)
            upper = jnp.where(lane == 0, jnp.where(row == 0, 0.0, before), upper)
            part[0, i, j] = lower + upper

    def exchange(i):
        return pltpu.make_async_remote_copy(
            src_ref=part.at[0, i], dst_ref=part.at[1, i],
            send_sem=part_sems.at[0, i], recv_sem=part_sems.at[1, i],
            device_id=partner, device_id_type=MESH)

    def push_first(i, carry):
        dx, rden, ub, own = (halves[0][k] for k in (0, 11, 12, 19))
        for j in range(4):
            slope = own[i, j] - smooth_time(ub[i, j]) * rden[i, j]
            own[i, j] = slope
            out_ref[i, j, :, :384] = slope[:, :384]
            raw[4 * i + j] = push(dx[i + 1, j + 1, :, :384], slope[:, :384], 0.0)
        return carry

    def push_second(i):
        dx, rden, ub, own = (halves[1][k] for k in (0, 11, 12, 19))
        for j in range(4):
            slope = own[i, j] - smooth_time(ub[i, j]) * rden[i, j]
            seam = jnp.where(lane < SEAM - 384, halves[0][19][i, j, :, 384:], slope[:, :128])
            slope = jnp.concatenate([seam, slope[:, 128:]], axis=1)
            out_ref[i, j, :, 384:] = slope
            raw[4 * i + j] = raw[4 * i + j] + push(dx[i + 1, j + 1], slope, 384.0)

    for turn, act in enumerate((first_turn, second_turn)):
        for n in (0, 1):
            when_all(rounds[2 * turn + n], 1, "wait_recv")
            act(n)
    when_all(rounds[4], 1, "wait_recv")
    smooth_space(halves[0][16], halves[0][17], halves[0][12])
    lax.fori_loop(0, 4, push_first, 0)
    when_all(rounds[5], 1, "wait_recv")
    smooth_space(halves[1][16], halves[1][17], halves[1][12])
    push_second(0)

    def push_rest(i, carry):
        gather(i - 1)
        push_second(i)
        exchange(i - 1).start()
        return carry

    lax.fori_loop(1, 4, push_rest, 0)
    gather(3)
    exchange(3).start()
    sums.wait_recv()
    weights = wsum[0] + wsum[1]
    for i in range(4):
        exchange(i).wait_recv()
        for j in range(4):
            stacked = (part[0, i, j] + part[1, i, j]) / weights
            for r in range(8):
                stack_ref[i, j:j + 1, 128 * r:128 * r + 128] = stacked[r:r + 1]
    sums.wait_send()
    for i in range(4):
        exchange(i).wait_send()
    for made in rounds:
        when_all(made, 0, "wait_send")


def moveout(data, offset_weight, counts):
    scratch = []
    for _, width in WINDOWS:
        tiles = pltpu.VMEM((6, 6, 8, width), jnp.float32)
        plane = pltpu.VMEM((6, 8, width), jnp.float32)
        own = pltpu.VMEM((4, 4, 8, width), jnp.float32)
        rows = pltpu.VMEM((4, 8, width), jnp.float32)
        scratch += [tiles, plane, plane, rows, rows, tiles, tiles, plane, plane, tiles, tiles,
                    own, own, own, tiles, plane, tiles, plane,
                    pltpu.VMEM((2, 4, 8, width), jnp.float32), own]
    return pl.pallas_call(
        lambda *refs: moveout_kernel(counts, *refs),
        out_shape=(jax.ShapeDtypeStruct((4, 4, 8, T), jnp.float32),
                   jax.ShapeDtypeStruct((4, 4, T), jnp.float32)),
        in_specs=[pl.BlockSpec(memory_space=pltpu.HBM)] * 2,
        out_specs=(pl.BlockSpec(memory_space=pltpu.VMEM), pl.BlockSpec(memory_space=pltpu.VMEM)),
        scratch_shapes=scratch + [
            pltpu.VMEM((2, 8, 128), jnp.float32),
            pltpu.VMEM((16, 4 * NA, NB), jnp.float32),
            pltpu.VMEM((2, 4, 4, 8, 128), jnp.float32),
            pltpu.SMEM((8,), jnp.float32), pltpu.SemaphoreType.DMA,
            pltpu.SemaphoreType.DMA((2,)), pltpu.SemaphoreType.DMA((6, 27)),
            pltpu.SemaphoreType.DMA((6, 27)), pltpu.SemaphoreType.DMA((2,)),
            pltpu.SemaphoreType.DMA((2, 4))],
        compiler_params=pltpu.CompilerParams(
            collective_id=0, has_side_effects=True, vmem_limit_bytes=48 * 2**20),
        name="moveout",
    )(pltpu.with_memory_space_constraint(offset_weight, pltpu.HBM),
      pltpu.with_memory_space_constraint(data, pltpu.HBM))


def solution(mesh):
    counts = (mesh.shape["il"], mesh.shape["xl"])
    return jax.shard_map(
        lambda data, offset_weight: moveout(data, offset_weight, counts),
        mesh=mesh,
        in_specs=(P("il", "xl", "off", None), P("off")),
        out_specs=(P("il", "xl", "off", None), P("il", "xl", None)),
        check_vma=False,
    )
```

time: 58.7 us -> 51.5 us (0.88)
  the two profiles are of different devices: /device:TPU:18 before, /device:TPU:2 now
where the time goes in v4:
time: 51.5 us; the launch traced here: 51.3 us
  Pallas kernels  49.3 us (96%)
  local copies, waits for them, and re-layouts  1.42 us (3%)
  between operations  0.64 us (1%)
    pallas_call x1, Pallas kernels, moveout(): pl.pallas_call(lambda *refs: moveout_kernel(counts, *refs), out_shape=(ja...  49.3 us
    unnamed x2, local copies, waits for them, and re-layouts  1.42 us

profile of v4, /device:TPU:2, one launch (start us, length us, event | category | flops | bytes accessed | tf_op | source)
XLA Modules:
  0.0 51.3 jit_solution(15195257889739727207)
XLA Ops:
  0.6 49.3 %moveout.1 = (f32[4,4,8,1024]{3,2,1,0:T(8,128)S(1)}, f32[4,4,1024]{2,1,0:T(4,128)S(1)}) custom-call(f32[8]{0:T(128)} %refs_0_.1, f32[4,4,8,1024]{3,2,1,0:T(8,128)} %refs_1_.1), custom_call_target="tpu_custom_call" | custom-call | tf_op jit(solution)/shard_map/moveout/pallas_call | solution.py:364
  49.9 0.8 %copy.6 = f32[4,4,8,1024]{3,2,1,0:T(8,128)} copy(f32[4,4,8,1024]{3,2,1,0:T(8,128)S(1)} %get-tuple-element.4) | data formatting | bytes 1048576
  50.7 0.6 %copy.7 = f32[4,4,1024]{2,1,0:T(4,128)} copy(f32[4,4,1024]{2,1,0:T(4,128)S(1)} %get-tuple-element.5) | data formatting | bytes 131072

commit v5 on v4

--- a/solution.py
+++ b/solution.py
@@ -51,30 +51,34 @@
     def transfers(turn, field, planes):
         made = []
         for k, (di, dj) in enumerate(STEPS):
-            kinds = []
-            if (di, dj) != (0, 0):
-                kinds.append((k, off, None, field.at[INNER[di], INNER[dj]],
-                              field.at[TARGET[di], TARGET[dj]]))
-            for n, (source, target, sender) in enumerate(planes):
-                kinds.append((9 + 9 * n + k, 1 - off, sender, source.at[SOURCE[di], SOURCE[dj]],
-                              target.at[TARGET[di], TARGET[dj]]))
-            for slot, to_off, sender, source, target in kinds:
-                copy = pltpu.make_async_remote_copy(
+            def copy(slot, to_off, source, target):
+                return pltpu.make_async_remote_copy(
                     src_ref=source, dst_ref=target,
                     send_sem=send_sems.at[turn, slot], recv_sem=recv_sems.at[turn, slot],
                     device_id={"off": to_off, "il": il + di, "xl": xl + dj},
                     device_id_type=MESH)
-                sends, takes = exists(di, dj), exists(-di, -dj)
-                if sender is not None:
-                    sends, takes = sends & (off == sender), takes & (off == 1 - sender)
-                made.append((sends, takes, copy))
+            sends, takes = exists(di, dj), exists(-di, -dj)
+            copies = []
+            if field is not None and (di, dj) != (0, 0):
+                copies.append(copy(k, off, field.at[INNER[di], INNER[dj]],
+                                   field.at[TARGET[di], TARGET[dj]]))
+            for n, (source, target) in enumerate(planes):
+                plane = copy(9 + 9 * n + k, 1 - off, source.at[SOURCE[di], SOURCE[dj]],
+                             target.at[TARGET[di], TARGET[dj]])
+                if n == 0:
+                    copies.append(plane)
+                else:
+                    made.append((sends & (off == 1), takes & first, [plane], 18 + k))
+            if copies:
+                made.append((sends, takes, copies, 9 + k))
         return made
 
     def when_all(made, which, act):
         for item in made:
             @pl.when(item[which])
             def _():
-                getattr(item[2], act)()
+                for copy in item[2]:
+                    getattr(copy, act)()
 
     loads = []
     for n, (base, width) in enumerate(WINDOWS):
@@ -96,42 +100,41 @@
     rows_near = 1 + (il > 0).astype(jnp.int32) + (il < n_il - 1).astype(jnp.int32)
     cols_near = 1 + (xl > 0).astype(jnp.int32) + (xl < n_xl - 1).astype(jnp.int32)
 
-    for dx, d0, d1, _, _, gg, gr, hgg, hgr, grad, res, rden, ub, uc, q2, o2, q3, o3, pq, own \
-            in halves:
-        for field, planes in ((dx, (d0, d1)), (q2, (o2,)), (q3, (o3,))):
-            for di, dj in STEPS:
-                if (di, dj) != (0, 0):
-                    @pl.when(jnp.logical_not(exists(-di, -dj)))
-                    def _():
-                        for target in (field,) + planes:
-                            shape = target.at[TARGET[di], TARGET[dj]].shape
-                            target[TARGET[di], TARGET[dj]] = jnp.zeros(shape, jnp.float32)
-
     load_weight.wait()
     total = weight_ref[0]
     for h in range(1, 8):
         total = total + weight_ref[h]
     wsum[0] = jnp.full((8, 128), total, jnp.float32)
-    for load, half in zip(loads, halves):
+    for load in loads:
         load.wait()
-        dx, p0, p1 = half[0], half[3], half[4]
+    pl.semaphore_wait(barrier, 2 * rows_near * cols_near - 1)
+
+    rounds = []
+    for n, half in enumerate(halves):
+        dx, d0, d1, p0, p1 = half[:5]
+        made = transfers(n, dx, [])
+        when_all(made, 0, "start")
         for i in range(4):
             for j in range(4):
                 tile = dx[1 + i, 1 + j]
                 p0[i, j:j + 1] = jnp.where(first, tile[7:8], tile[0:1])
                 p1[i, j:j + 1] = tile[1:2]
-    pl.semaphore_wait(barrier, 2 * rows_near * cols_near - 1)
-
-    rounds = []
-    for n, half in enumerate(halves):
-        dx, d0, d1, p0, p1 = half[:5]
-        made = transfers(n, dx, [(p0, d0, None), (p1, d1, 1)])
-        when_all(made, 0, "start")
-        rounds.append(made)
+        plane = transfers(n, None, [(p0, d0), (p1, d1)])
+        when_all(plane, 0, "start")
+        rounds.append((made, plane))
     sums = pltpu.make_async_remote_copy(
         src_ref=wsum.at[0], dst_ref=wsum.at[1], send_sem=sum_sems.at[0], recv_sem=sum_sems.at[1],
         device_id=partner, device_id_type=MESH)
     sums.start()
+
+    for di, dj in STEPS:
+        if (di, dj) != (0, 0):
+            @pl.when(jnp.logical_not(exists(-di, -dj)))
+            def _():
+                for half in halves:
+                    for n in (0, 1, 2, 14, 15, 16, 17):
+                        shape = half[n].at[TARGET[di], TARGET[dj]].shape
+                        half[n][TARGET[di], TARGET[dj]] = jnp.zeros(shape, jnp.float32)
 
     keep_next = jnp.where(first, 1.0, 0.0)
     keep_before = 1.0 - keep_next
@@ -162,11 +165,33 @@
             return carry
         lax.fori_loop(0, field.shape[3] // 128, column, 0)
 
-    def first_turn(n):
+    def first_turn(n, inner):
         dx, d0, d1, _, _, gg, gr, hgg, hgr, grad, res, rden, ub, uc, q2, o2, q3, o3, pq, own = \
             halves[n]
         width = WINDOWS[n][1]
         row8 = lax.broadcasted_iota(jnp.int32, (8, width), 0)
+
+        def gradients(i, j):
+            d = dx[i, j]
+            edge = jnp.broadcast_to(d0[i, j:j + 1] * keep_next, (8, width))
+            f = jnp.where(row8 == 7, edge, pltpu.roll(d, 7, 0))
+            r = f - d
+            s = d + f
+            g = 0.25 * (later(s, 1) - earlier(s, 1))
+            gg[i, j] = g * g
+            gr[i, j] = g * r
+            grad[i, j] = g
+            res[i, j] = r
+
+        made, plane = rounds[n]
+        if inner:
+            centre = [item for item in plane if item[3] == 13]
+            when_all(centre, 1, "wait_recv")
+            for i in range(1, 5):
+                for j in range(1, 5):
+                    gradients(i, j)
+            return
+        when_all(made + [item for item in plane if item[3] != 13], 1, "wait_recv")
 
         @pl.when(off == 1)
         def _():
@@ -174,26 +199,16 @@
                 for j in range(6):
                     d1[i, j:j + 1] = dx[i, j, 0:1]
 
-        def gradients(i, carry):
+        for i in range(6):
             for j in range(6):
-                d = dx[i, j]
-                edge = jnp.broadcast_to(d0[i, j:j + 1] * keep_next, (8, width))
-                f = jnp.where(row8 == 7, edge, pltpu.roll(d, 7, 0))
-                r = f - d
-                s = d + f
-                g = 0.25 * (later(s, 1) - earlier(s, 1))
-                gg[i, j] = g * g
-                gr[i, j] = g * r
-                grad[i, j] = g
-                res[i, j] = r
+                if i in (0, 5) or j in (0, 5):
+                    gradients(i, j)
             d, f = d0[i], d1[i]
             s = d + f
             g = 0.25 * (later(s, 1) - earlier(s, 1))
             hgg[i] = g * g
             hgr[i] = g * (f - d)
-            return carry
-
-        lax.fori_loop(0, 6, gradients, 0)
+
         smooth_space(gg, hgg, ub)
         smooth_space(gr, hgr, uc)
 
@@ -209,8 +224,8 @@
                 pq[0, i, j:j + 1] = jnp.where(first, q[7:8], q[0:1])
             return carry
 
-        lax.fori_loop(0, 4, start_slope, 0)
-        made = transfers(2 + n, q2, [(pq.at[0], o2, None)])
+        lax.fori_loop(0, 4, start_slope, 0, unroll=2)
+        made = transfers(2 + n, q2, [(pq.at[0], o2)])
         when_all(made, 0, "start")
         rounds.append(made)
 
@@ -229,8 +244,8 @@
                 pq[1, i, j:j + 1] = jnp.where(first, q[7:8], q[0:1])
             return carry
 
-        lax.fori_loop(0, 4, next_slope, 0)
-        made = transfers(4 + n, q3, [(pq.at[1], halves[n][17], None)])
+        lax.fori_loop(0, 4, next_slope, 0, unroll=4)
+        made = transfers(4 + n, q3, [(pq.at[1], halves[n][17])])
         when_all(made, 0, "start")
         rounds.append(made)
 
@@ -316,13 +331,21 @@
             out_ref[i, j, :, 384:] = slope
             raw[4 * i + j] = raw[4 * i + j] + push(dx[i + 1, j + 1], slope, 384.0)
 
-    for turn, act in enumerate((first_turn, second_turn)):
-        for n in (0, 1):
-            when_all(rounds[2 * turn + n], 1, "wait_recv")
-            act(n)
+    first_turn(0, True)
+    first_turn(1, True)
+    first_turn(0, False)
+    first_turn(1, False)
+    for made in rounds[0] + rounds[1]:
+        when_all(made, 0, "wait_send")
+    for n in (0, 1):
+        when_all(rounds[2 + n], 1, "wait_recv")
+        second_turn(n)
+    for made in rounds[2:4]:
+        when_all(made, 0, "wait_send")
     when_all(rounds[4], 1, "wait_recv")
     smooth_space(halves[0][16], halves[0][17], halves[0][12])
     lax.fori_loop(0, 4, push_first, 0)
+    when_all(rounds[4], 0, "wait_send")
     when_all(rounds[5], 1, "wait_recv")
     smooth_space(halves[1][16], halves[1][17], halves[1][12])
     push_second(0)
@@ -336,6 +359,7 @@
     lax.fori_loop(1, 4, push_rest, 0)
     gather(3)
     exchange(3).start()
+    when_all(rounds[5], 0, "wait_send")
     sums.wait_recv()
     weights = wsum[0] + wsum[1]
     for i in range(4):
@@ -347,8 +371,6 @@
     sums.wait_send()
     for i in range(4):
         exchange(i).wait_send()
-    for made in rounds:
-        when_all(made, 0, "wait_send")
 
 
 def moveout(data, offset_weight, counts):

time: 51.5 us -> 52.1 us (1.012)
  the two profiles are of different devices: /device:TPU:2 before, /device:TPU:26 now
where the time goes in v5:
time: 52.1 us; the launch traced here: 51.9 us
  Pallas kernels  49.9 us (96%)
  local copies, waits for them, and re-layouts  1.42 us (3%)
  between operations  0.64 us (1%)
    pallas_call x1, Pallas kernels, moveout(): pl.pallas_call(lambda *refs: moveout_kernel(counts, *refs), out_shape=(ja...  49.9 us
    unnamed x2, local copies, waits for them, and re-layouts  1.42 us

profile of v5, /device:TPU:26, one launch (start us, length us, event | category | flops | bytes accessed | tf_op | source)
XLA Modules:
  0.0 51.9 jit_solution(8238499000203727136)
XLA Ops:
  0.6 49.9 %moveout.1 = (f32[4,4,8,1024]{3,2,1,0:T(8,128)S(1)}, f32[4,4,1024]{2,1,0:T(4,128)S(1)}) custom-call(f32[8]{0:T(128)} %refs_0_.1, f32[4,4,8,1024]{3,2,1,0:T(8,128)} %refs_1_.1), custom_call_target="tpu_custom_call" | custom-call | tf_op jit(solution)/shard_map/moveout/pallas_call | solution.py:386
  50.5 0.8 %copy.6 = f32[4,4,8,1024]{3,2,1,0:T(8,128)} copy(f32[4,4,8,1024]{3,2,1,0:T(8,128)S(1)} %get-tuple-element.4) | data formatting | bytes 1048576
  51.3 0.6 %copy.7 = f32[4,4,1024]{2,1,0:T(4,128)} copy(f32[4,4,1024]{2,1,0:T(4,128)S(1)} %get-tuple-element.5) | data formatting | bytes 131072

commit v6 on v5

--- a/solution.py
+++ b/solution.py
@@ -10,7 +10,8 @@
 NB = 64
 damping = 0.05
 MESH = pl.DeviceIdType.MESH
-STEPS = [(di, dj) for di in (-1, 0, 1) for dj in (-1, 0, 1)]
+STEPS = [(-1, -1), (-1, 1), (1, -1), (1, 1), (0, -1), (0, 1), (0, 0), (-1, 0), (1, 0)]
+CENTRE = 9 + STEPS.index((0, 0))
 SOURCE = {-1: slice(0, 1), 0: slice(0, 4), 1: slice(3, 4)}
 INNER = {-1: slice(1, 2), 0: slice(1, 5), 1: slice(4, 5)}
 TARGET = {-1: slice(5, 6), 0: slice(1, 5), 1: slice(0, 1)}
@@ -38,7 +39,7 @@
 def moveout_kernel(counts, weight_hbm, data_hbm, out_ref, stack_ref, *scratch):
     halves, scratch = (scratch[:20], scratch[20:40]), scratch[40:]
     (wsum, raw, part, weight_ref, weight_sem, load_sems, send_sems, recv_sems,
-     sum_sems, part_sems) = scratch
+     sum_sems, part_sems, seam_inner) = scratch
     n_il, n_xl = counts
     off, il, xl = lax.axis_index("off"), lax.axis_index("il"), lax.axis_index("xl")
     first = off == 0
@@ -165,6 +166,23 @@
             return carry
         lax.fori_loop(0, field.shape[3] // 128, column, 0)
 
+    def smooth_inner(field, out):
+        def column(c, carry):
+            lanes = pl.ds(pl.multiple_of(c * 128, 128), 128)
+            sums_xl = []
+            for i in range(1, 5):
+                tiles = [field[i, j, :, lanes] for j in range(1, 5)]
+                pairs = [tiles[j] + tiles[j + 1] for j in range(3)]
+                sums_xl.append([pairs[j] + pairs[j + 1] for j in range(2)])
+            for i in range(2):
+                for j in range(2):
+                    x = sums_xl[i][j] + 2.0 * sums_xl[i + 1][j] + sums_xl[i + 2][j]
+                    up = jnp.where(row == 0, 0.0, pltpu.roll(x, 1, 0))
+                    down = jnp.where(row == 7, 0.0, pltpu.roll(x, 7, 0))
+                    out[1 + i, 1 + j, :, lanes] = up + 2.0 * x + down
+            return carry
+        lax.fori_loop(0, field.shape[3] // 128, column, 0)
+
     def first_turn(n, inner):
         dx, d0, d1, _, _, gg, gr, hgg, hgr, grad, res, rden, ub, uc, q2, o2, q3, o3, pq, own = \
             halves[n]
@@ -185,13 +203,13 @@
 
         made, plane = rounds[n]
         if inner:
-            centre = [item for item in plane if item[3] == 13]
+            centre = [item for item in plane if item[3] == CENTRE]
             when_all(centre, 1, "wait_recv")
             for i in range(1, 5):
                 for j in range(1, 5):
                     gradients(i, j)
             return
-        when_all(made + [item for item in plane if item[3] != 13], 1, "wait_recv")
+        when_all(made + [item for item in plane if item[3] != CENTRE], 1, "wait_recv")
 
         @pl.when(off == 1)
         def _():
@@ -252,6 +270,8 @@
     weight = jnp.full((8, 128), weight_ref[0], jnp.float32)
     for h in range(1, 8):
         weight = jnp.where(row == h, weight_ref[h], weight)
+    edge_row = jnp.where(first, 7, 0)
+    inner_weight = jnp.where(row == edge_row, 0.0, weight)
     high = lax.broadcasted_iota(jnp.int32, (NA, 128), 0)
     high = jnp.where(high < 8, 2 * high, 2 * high - 15)
     high = high.astype(jnp.float32).astype(jnp.bfloat16)
@@ -260,7 +280,7 @@
     zero_b = jnp.zeros((NB, 128), jnp.bfloat16)
     one_b = jnp.ones((NB, 128), jnp.bfloat16)
 
-    def push(data, slope, start):
+    def push(data, slope, start, kind="full"):
         width = data.shape[1]
         tt = lax.broadcasted_iota(jnp.int32, (8, width), 1).astype(jnp.float32) + (start + 1.0)
         hh = lax.broadcasted_iota(jnp.int32, (8, width), 0).astype(jnp.float32) + 0.5
@@ -271,16 +291,21 @@
         cell = jnp.minimum(cell, float(T))
         a = jnp.floor(cell * (1.0 / NB))
         b = cell - a * NB
-        v = data * jnp.concatenate([weight] * (width // 128), axis=1)
+        scale = inner_weight if kind == "inner" else weight
+        v = data * jnp.concatenate([scale] * (width // 128), axis=1)
         x1 = v * f
         x0 = v - x1
         x0h = x0.astype(jnp.bfloat16).astype(jnp.float32)
         x1h = x1.astype(jnp.bfloat16).astype(jnp.float32)
         values = (x0h, x0 - x0h, x1h, x1 - x1h)
+        groups = [(h, h + 1) for h in range(0, 8, 2)]
+        if kind == "edge":
+            a, b, *values = [jnp.where(first, x[7:8], x[0:1]) for x in (a, b) + values]
+            groups = [(0,)]
         acc = jnp.zeros((4 * NA, NB), jnp.float32)
-        for h in range(0, 8, 2):
+        for group in groups:
             left, right = [], []
-            for k in (h, h + 1):
+            for k in group:
                 for c in range(0, width, 128):
                     def spread(x, n):
                         piece = x[k:k + 1, c:c + 128]
@@ -313,50 +338,82 @@
             send_sem=part_sems.at[0, i], recv_sem=part_sems.at[1, i],
             device_id=partner, device_id_type=MESH)
 
-    def push_first(i, carry):
-        dx, rden, ub, own = (halves[0][k] for k in (0, 11, 12, 19))
-        for j in range(4):
-            slope = own[i, j] - smooth_time(ub[i, j]) * rden[i, j]
-            own[i, j] = slope
+    def last_slope(n, i, j):
+        rden, ub, own = (halves[n][k] for k in (11, 12, 19))
+        return own[i, j] - smooth_time(ub[i, j]) * rden[i, j]
+
+    def push_first(i, j, kind):
+        slope = last_slope(0, i, j)
+        added = push(halves[0][0][i + 1, j + 1, :, :384], slope[:, :384], 0.0, kind)
+        if kind == "inner":
+            seam_inner[i - 1, j - 1] = slope[:, 384:]
+        else:
+            halves[0][19][i, j] = slope
             out_ref[i, j, :, :384] = slope[:, :384]
-            raw[4 * i + j] = push(dx[i + 1, j + 1, :, :384], slope[:, :384], 0.0)
-        return carry
-
-    def push_second(i):
-        dx, rden, ub, own = (halves[1][k] for k in (0, 11, 12, 19))
-        for j in range(4):
-            slope = own[i, j] - smooth_time(ub[i, j]) * rden[i, j]
-            seam = jnp.where(lane < SEAM - 384, halves[0][19][i, j, :, 384:], slope[:, :128])
-            slope = jnp.concatenate([seam, slope[:, 128:]], axis=1)
+        if kind == "edge":
+            added = raw[4 * i + j] + added
+        raw[4 * i + j] = added
+
+    def push_second(i, j, kind):
+        slope = last_slope(1, i, j)
+        before = seam_inner[i - 1, j - 1] if kind == "inner" else halves[0][19][i, j, :, 384:]
+        seam = jnp.where(lane < SEAM - 384, before, slope[:, :128])
+        slope = jnp.concatenate([seam, slope[:, 128:]], axis=1)
+        if kind != "inner":
             out_ref[i, j, :, 384:] = slope
-            raw[4 * i + j] = raw[4 * i + j] + push(dx[i + 1, j + 1], slope, 384.0)
-
-    first_turn(0, True)
-    first_turn(1, True)
-    first_turn(0, False)
-    first_turn(1, False)
+        added = push(halves[1][0][i + 1, j + 1], slope, 384.0, kind)
+        raw[4 * i + j] = raw[4 * i + j] + added
+
+    inner = [(i, j) for i in (1, 2) for j in (1, 2)]
+    sides = [(i, j) for i in (1, 2) for j in (0, 3)]
+
+    for n in (0, 1):
+        first_turn(n, True)
+        first_turn(n, False)
     for made in rounds[0] + rounds[1]:
         when_all(made, 0, "wait_send")
     for n in (0, 1):
         when_all(rounds[2 + n], 1, "wait_recv")
         second_turn(n)
+    smooth_inner(halves[0][16], halves[0][12])
+    for i, j in inner:
+        push_first(i, j, "inner")
+    smooth_inner(halves[1][16], halves[1][12])
+    for i, j in inner:
+        push_second(i, j, "inner")
     for made in rounds[2:4]:
         when_all(made, 0, "wait_send")
+
     when_all(rounds[4], 1, "wait_recv")
     smooth_space(halves[0][16], halves[0][17], halves[0][12])
-    lax.fori_loop(0, 4, push_first, 0)
+
+    def push_row(k, carry):
+        for j in range(4):
+            push_first(3 * k, j, "full")
+        return carry
+
+    lax.fori_loop(0, 2, push_row, 0)
+    for i, j in sides:
+        push_first(i, j, "full")
+    for i, j in inner:
+        push_first(i, j, "edge")
     when_all(rounds[4], 0, "wait_send")
     when_all(rounds[5], 1, "wait_recv")
     smooth_space(halves[1][16], halves[1][17], halves[1][12])
-    push_second(0)
-
-    def push_rest(i, carry):
-        gather(i - 1)
-        push_second(i)
-        exchange(i - 1).start()
-        return carry
-
-    lax.fori_loop(1, 4, push_rest, 0)
+    for j in range(4):
+        push_second(0, j, "full")
+    gather(0)
+    for i, j in sides:
+        push_second(i, j, "full")
+    for i, j in inner:
+        push_second(i, j, "edge")
+    exchange(0).start()
+    gather(1)
+    gather(2)
+    for j in range(4):
+        push_second(3, j, "full")
+    exchange(1).start()
+    exchange(2).start()
     gather(3)
     exchange(3).start()
     when_all(rounds[5], 0, "wait_send")
@@ -396,7 +453,7 @@
             pltpu.SMEM((8,), jnp.float32), pltpu.SemaphoreType.DMA,
             pltpu.SemaphoreType.DMA((2,)), pltpu.SemaphoreType.DMA((6, 27)),
             pltpu.SemaphoreType.DMA((6, 27)), pltpu.SemaphoreType.DMA((2,)),
-            pltpu.SemaphoreType.DMA((2, 4))],
+            pltpu.SemaphoreType.DMA((2, 4)), pltpu.VMEM((2, 2, 8, 128), jnp.float32)],
         compiler_params=pltpu.CompilerParams(
             collective_id=0, has_side_effects=True, vmem_limit_bytes=48 * 2**20),
         name="moveout",

time: 52.1 us -> 48.4 us (0.929)
  the two profiles are of different devices: /device:TPU:26 before, /device:TPU:2 now
where the time goes in v6:
time: 48.4 us; the launch traced here: 48.3 us
  Pallas kernels  46.2 us (95%)
  local copies, waits for them, and re-layouts  1.42 us (3%)
  between operations  0.64 us (1%)
    pallas_call x1, Pallas kernels, moveout(): pl.pallas_call(lambda *refs: moveout_kernel(counts, *refs), out_shape=(ja...  46.2 us
    unnamed x2, local copies, waits for them, and re-layouts  1.42 us

profile of v6, /device:TPU:2, one launch (start us, length us, event | category | flops | bytes accessed | tf_op | source)
XLA Modules:
  0.0 48.3 jit_solution(8591068861151768783)
XLA Ops:
  0.6 46.2 %moveout.1 = (f32[4,4,8,1024]{3,2,1,0:T(8,128)S(1)}, f32[4,4,1024]{2,1,0:T(4,128)S(1)}) custom-call(f32[8]{0:T(128)} %refs_0_.1, f32[4,4,8,1024]{3,2,1,0:T(8,128)} %refs_1_.1), custom_call_target="tpu_custom_call" | custom-call | tf_op jit(solution)/shard_map/moveout/pallas_call | solution.py:443
  46.9 0.8 %copy.6 = f32[4,4,8,1024]{3,2,1,0:T(8,128)} copy(f32[4,4,8,1024]{3,2,1,0:T(8,128)S(1)} %get-tuple-element.4) | data formatting | bytes 1048576
  47.7 0.6 %copy.7 = f32[4,4,1024]{2,1,0:T(4,128)} copy(f32[4,4,1024]{2,1,0:T(4,128)S(1)} %get-tuple-element.5) | data formatting | bytes 131072

commit v7 on v6

--- a/solution.py
+++ b/solution.py
@@ -164,7 +164,7 @@
                     down = jnp.where(row == 7, down, pltpu.roll(x, 7, 0))
                     out[i, j, :, lanes] = up + 2.0 * x + down
             return carry
-        lax.fori_loop(0, field.shape[3] // 128, column, 0)
+        lax.fori_loop(0, field.shape[3] // 128, column, 0, unroll=True)
 
     def smooth_inner(field, out):
         def column(c, carry):
@@ -181,7 +181,7 @@
                     down = jnp.where(row == 7, 0.0, pltpu.roll(x, 7, 0))
                     out[1 + i, 1 + j, :, lanes] = up + 2.0 * x + down
             return carry
-        lax.fori_loop(0, field.shape[3] // 128, column, 0)
+        lax.fori_loop(0, field.shape[3] // 128, column, 0, unroll=True)
 
     def first_turn(n, inner):
         dx, d0, d1, _, _, gg, gr, hgg, hgr, grad, res, rden, ub, uc, q2, o2, q3, o3, pq, own = \
@@ -242,7 +242,7 @@
                 pq[0, i, j:j + 1] = jnp.where(first, q[7:8], q[0:1])
             return carry
 
-        lax.fori_loop(0, 4, start_slope, 0, unroll=2)
+        lax.fori_loop(0, 4, start_slope, 0, unroll=True)
         made = transfers(2 + n, q2, [(pq.at[0], o2)])
         when_all(made, 0, "start")
         rounds.append(made)

time: 48.4 us -> 47.8 us (0.988)
  the two profiles are of different devices: /device:TPU:2 before, /device:TPU:18 now
where the time goes in v7:
time: 47.8 us; the launch traced here: 47.6 us
  Pallas kernels  45.6 us (95%)
  local copies, waits for them, and re-layouts  1.42 us (3%)
  between operations  0.64 us (1%)
    pallas_call x1, Pallas kernels, moveout(): pl.pallas_call(lambda *refs: moveout_kernel(counts, *refs), out_shape=(ja...  45.6 us
    unnamed x2, local copies, waits for them, and re-layouts  1.42 us

profile of v7, /device:TPU:18, one launch (start us, length us, event | category | flops | bytes accessed | tf_op | source)
XLA Modules:
  0.0 47.6 jit_solution(15055170363365044301)
XLA Ops:
  0.6 45.6 %moveout.1 = (f32[4,4,8,1024]{3,2,1,0:T(8,128)S(1)}, f32[4,4,1024]{2,1,0:T(4,128)S(1)}) custom-call(f32[8]{0:T(128)} %refs_0_.1, f32[4,4,8,1024]{3,2,1,0:T(8,128)} %refs_1_.1), custom_call_target="tpu_custom_call" | custom-call | tf_op jit(solution)/shard_map/moveout/pallas_call | solution.py:443
  46.2 0.8 %copy.6 = f32[4,4,8,1024]{3,2,1,0:T(8,128)} copy(f32[4,4,8,1024]{3,2,1,0:T(8,128)S(1)} %get-tuple-element.4) | data formatting | bytes 1048576
  47.0 0.6 %copy.7 = f32[4,4,1024]{2,1,0:T(4,128)} copy(f32[4,4,1024]{2,1,0:T(4,128)S(1)} %get-tuple-element.5) | data formatting | bytes 131072

commit v8 on v7

--- a/solution.py
+++ b/solution.py
@@ -106,8 +106,14 @@
     for h in range(1, 8):
         total = total + weight_ref[h]
     wsum[0] = jnp.full((8, 128), total, jnp.float32)
-    for load in loads:
+    for load, half in zip(loads, halves):
         load.wait()
+        dx, p0, p1 = half[0], half[3], half[4]
+        for i in range(4):
+            for j in range(4):
+                tile = dx[1 + i, 1 + j]
+                p0[i, j:j + 1] = jnp.where(first, tile[7:8], tile[0:1])
+                p1[i, j:j + 1] = tile[1:2]
     pl.semaphore_wait(barrier, 2 * rows_near * cols_near - 1)
 
     rounds = []
@@ -115,11 +121,6 @@
         dx, d0, d1, p0, p1 = half[:5]
         made = transfers(n, dx, [])
         when_all(made, 0, "start")
-        for i in range(4):
-            for j in range(4):
-                tile = dx[1 + i, 1 + j]
-                p0[i, j:j + 1] = jnp.where(first, tile[7:8], tile[0:1])
-                p1[i, j:j + 1] = tile[1:2]
         plane = transfers(n, None, [(p0, d0), (p1, d1)])
         when_all(plane, 0, "start")
         rounds.append((made, plane))

time: 47.8 us -> 47.7 us (level)
  no operation moved by 1% of the time
where the time goes in v8:
time: 47.7 us; the launch traced here: 47.6 us
  Pallas kernels  45.5 us (95%)
  local copies, waits for them, and re-layouts  1.42 us (3%)
  between operations  0.64 us (1%)
    pallas_call x1, Pallas kernels, moveout(): pl.pallas_call(lambda *refs: moveout_kernel(counts, *refs), out_shape=(ja...  45.5 us
    unnamed x2, local copies, waits for them, and re-layouts  1.42 us

profile of v8, /device:TPU:18, one launch (start us, length us, event | category | flops | bytes accessed | tf_op | source)
XLA Modules:
  0.0 47.6 jit_solution(15141702688730884717)
XLA Ops:
  0.6 45.5 %moveout.1 = (f32[4,4,8,1024]{3,2,1,0:T(8,128)S(1)}, f32[4,4,1024]{2,1,0:T(4,128)S(1)}) custom-call(f32[8]{0:T(128)} %refs_0_.1, f32[4,4,8,1024]{3,2,1,0:T(8,128)} %refs_1_.1), custom_call_target="tpu_custom_call" | custom-call | tf_op jit(solution)/shard_map/moveout/pallas_call | solution.py:444
  46.2 0.8 %copy.6 = f32[4,4,8,1024]{3,2,1,0:T(8,128)} copy(f32[4,4,8,1024]{3,2,1,0:T(8,128)S(1)} %get-tuple-element.4) | data formatting | bytes 1048576
  47.0 0.6 %copy.7 = f32[4,4,1024]{2,1,0:T(4,128)} copy(f32[4,4,1024]{2,1,0:T(4,128)S(1)} %get-tuple-element.5) | data formatting | bytes 131072
